TPU v7x, 128 devices: a whole 4x4x4 slice. The times are simulated.
128 devices in a mesh: ctx: 16 (over x_lo, z, core), mp: 4 (over y), rep: 2 (over x_hi).
Axes of the slice: x: 4 (x_hi: 2, x_lo: 2; x = x_hi * 2 + x_lo), y: 4, z: 4, core: 2. Of those that a mesh axis runs over, the one named last changes fastest.
Arguments:
- token_pages: bfloat16 [128, 128, 2048], P('ctx'), may hold values from -13 to 13
- page_table: int32 [128], P('ctx'), may hold values from 0 to 7, as said below
- live_flags: int32 [128], P('ctx'), may hold values from 0 to 1, as said below
- lengths: int32 [32], replicated, may hold values from 1 to 1024, as said below
- decay_floor: float32 [2048], P(('mp', 'rep')), may hold values from 0.85 to 0.9998
- mixer_gain: float32 [2048], replicated, may hold values from 0.5 to 1.5
- feed_gain: float32 [2048], replicated, may hold values from 0.5 to 1.5
- trainer_mixer_in: float32 [3, 2048, 2048], P(None, ('ctx', 'mp')), may hold values from -0.125 to 0.125
- trainer_mixer_out: float32 [2048, 2048], P(None, ('ctx', 'mp')), may hold values from -0.125 to 0.125
- trainer_gate_up: float32 [2, 2048, 5632], P(None, ('ctx', 'mp')), may hold values from -0.125 to 0.125
- trainer_down: float32 [5632, 2048], P(None, ('ctx', 'mp')), may hold values from -0.078125 to 0.078125
Outputs:
- layer_output: bfloat16 [16384, 2048], P(('ctx', 'rep'), 'mp')
Inputs may be any that keep to these rules, and one draw needn't show every extreme that they name: `page_table`: within each device's block of 8 entries every value 0 to 7 appears once. `live_flags`: in each device's block of 8 flags at least half (rounded down, and never fewer than one) are ones, and some device's block is all ones. The lengths sum to 128 times the number of ones in live_flags; one prompt has exactly 1024 tokens.
All inputs are finite; a program needn't handle non-finite values.
Results may differ from a plain program's by a relative error of at most 0.015.
Values may be sent and summed in bfloat16 or wider, within the bound.
A program may use at most 192 MiB of HBM per device.

v0:
```python
import jax
import jax.numpy as jnp
from jax import lax
from jax.sharding import PartitionSpec as P

D = 2048
HEADS = 16


norm_eps = 1e-05


def prefix(value, axis, join, neutral):
    count, mine = (lax.axis_size(axis), lax.axis_index(axis))
    pieces = lax.all_gather(value, axis)
    total = jnp.full_like(value, 0) + jnp.asarray(neutral, value.dtype)

    def prefix_step(position, total):
        longer = join(total, pieces[position])
        return jnp.where(position < mine, longer, total)

    return lax.fori_loop(0, count - 1, prefix_step, total)


def entering_2(shard, axis, combine, identity):
    peers, position = (lax.axis_size(axis), lax.axis_index(axis))
    everything = jax.tree.map(
        lambda part, kind: lax.all_gather(part.astype(kind), axis),
        shard,
        (jnp.bfloat16, jnp.bfloat16),
    )
    start = jax.tree.map(
        lambda part, zero: jnp.broadcast_to(jnp.asarray(zero, part.dtype), part.shape),
        shard,
        identity,
    )

    def entering_step(k, before):
        reached = k < position
        new = combine(
            before, jax.tree.map(lambda part, own: part[k].astype(own.dtype), everything, shard)
        )
        return jax.tree.map(lambda a, b: jnp.where(reached, a, b), new, before)

    return lax.fori_loop(0, peers, entering_step, start)


def rms_scale(values_in, gain):
    mean_sq = jnp.mean(values_in * values_in, axis=-1, keepdims=True)
    return values_in * lax.rsqrt(mean_sq + norm_eps) * gain


def block_recurrence(queries, keys_in, values_in, log_decay, reset_count, state_init, count_init):
    highest = lax.Precision.HIGHEST

    def advance(carried_in, block_data):
        state, count_before = carried_in
        q_block, k_block, v_block, decay_block, count_block = block_data
        cumulative = jnp.cumsum(decay_block, axis=0)
        q_scaled = q_block * jnp.exp(cumulative)
        k_scaled = k_block * jnp.exp(-cumulative)
        scores = jnp.einsum("thd,shd->hts", q_scaled, k_scaled, precision=highest)
        positions = jnp.arange(count_block.shape[0])
        allowed = (positions[:, None] >= positions[None, :]) & (
            count_block[:, None] == count_block[None, :]
        )
        scores = jnp.where(allowed[None], scores, 0.0)
        outputs = jnp.einsum("hts,shd->thd", scores, v_block, precision=highest)
        from_state = jnp.einsum("thd,hde->the", q_scaled, state, precision=highest)
        outputs = outputs + jnp.where((count_block == count_before)[:, None, None], from_state, 0.0)
        last_count = count_block[-1]
        final_cum = cumulative[-1]
        weight_keys = (
            k_block
            * jnp.exp(final_cum[None] - cumulative)
            * (count_block == last_count).astype(k_block.dtype)[:, None, None]
        )
        retained = jnp.where(
            last_count == count_before, jnp.exp(final_cum)[:, :, None] * state, 0.0
        )
        state_next = retained + jnp.einsum("thd,the->hde", weight_keys, v_block, precision=highest)
        return ((state_next, last_count), outputs)

    final_carry, outputs_all = lax.scan(
        advance, (state_init, count_init), (queries, keys_in, values_in, log_decay, reset_count)
    )
    return (outputs_all, final_carry[0])


def compose_states(earlier, later):
    return (earlier[0] * later[0], later[0][:, :, None] * earlier[1] + later[1])


def add_counts(earlier, later):
    return earlier + later


def shards(
    token_pages,
    page_table,
    live_flags,
    lengths,
    decay_floor,
    mixer_gain,
    feed_gain,
    trainer_mixer_in,
    trainer_mixer_out,
    trainer_gate_up,
    trainer_down,
):
    mp_count = lax.axis_size("mp")
    rep_count = lax.axis_size("rep")
    mp_index = lax.axis_index("mp")
    rep_index = lax.axis_index("rep")
    width_local = trainer_mixer_in.shape[1]
    model_width = trainer_mixer_in.shape[2]
    head_cols = decay_floor.shape[0]
    head_dim = D // HEADS
    local_heads = head_cols // head_dim
    hidden_block = trainer_gate_up.shape[2] // mp_count
    mixer_in = lax.dynamic_index_in_dim(
        trainer_mixer_in.reshape(3, width_local, mp_count, rep_count, head_cols),
        rep_index,
        3,
        keepdims=False,
    )
    mixer_in = jnp.transpose(mixer_in, (1, 2, 0, 3)).reshape(width_local, mp_count, 3 * head_cols)
    mixer_out = lax.dynamic_index_in_dim(
        trainer_mixer_out.reshape(mp_count, rep_count, head_cols, width_local),
        rep_index,
        1,
        keepdims=False,
    )
    mixer_out = jnp.transpose(mixer_out, (2, 0, 1))
    gate_up = trainer_gate_up.reshape(2, width_local, mp_count, hidden_block)
    down_rows = trainer_down.reshape(mp_count, hidden_block, width_local)
    gate_up = jnp.transpose(gate_up, (1, 2, 0, 3)).reshape(width_local, mp_count, 2 * hidden_block)
    down_rows = jnp.transpose(down_rows, (2, 0, 1))
    packed = jnp.concatenate([mixer_in, mixer_out, gate_up, down_rows], axis=2).astype(jnp.bfloat16)
    arrived = lax.all_to_all(packed, "mp", split_axis=1, concat_axis=0, tiled=True)
    arrived = arrived.reshape(mp_count * width_local, packed.shape[2])
    served = lax.all_gather(arrived, "ctx", axis=0, tiled=True)
    w_mixer = served[:, : 3 * head_cols]
    w_output_t = served[:, 3 * head_cols : 4 * head_cols]
    feed_weights = served[:, 4 * head_cols :].reshape(model_width, 3, hidden_block)
    pages_local = token_pages.shape[0]
    page_len = token_pages.shape[1]
    tok_count = pages_local * page_len
    ordered = jnp.take(token_pages, page_table, axis=0).reshape(tok_count, model_width)
    live_tokens = jnp.repeat(live_flags, page_len)
    page_live = live_flags * page_len
    live_total = jnp.sum(page_live)
    stream_base = prefix(live_total, "ctx", add_counts, jnp.zeros((), jnp.int32))
    page_start = stream_base + jnp.cumsum(page_live) - page_live
    positions = (page_start[:, None] + jnp.arange(page_len, dtype=jnp.int32)[None, :]).reshape(
        tok_count
    )
    starts = jnp.cumsum(lengths) - lengths
    resets = (live_tokens == 1) & jnp.any(positions[:, None] == starts[None, :], axis=1)
    reset_count = jnp.cumsum(resets.astype(jnp.int32))
    live_float = live_tokens.astype(jnp.float32)[:, None]
    normed = rms_scale(ordered.astype(jnp.float32), mixer_gain).astype(jnp.bfloat16)
    projected = jnp.dot(normed, w_mixer, preferred_element_type=jnp.float32).reshape(
        tok_count, 3, head_cols
    )
    queries = jax.nn.silu(projected[:, 0])
    forget = decay_floor + (1.0 - decay_floor) * jax.nn.sigmoid(projected[:, 1])
    log_decay = jnp.log(forget) * live_float
    keys_in = (1.0 - forget) * live_float
    values_in = projected[:, 2]
    shape_blocks = (pages_local, page_len, local_heads, head_dim)
    local_out, local_state = block_recurrence(
        queries.reshape(shape_blocks),
        keys_in.reshape(shape_blocks),
        values_in.reshape(shape_blocks),
        log_decay.reshape(shape_blocks),
        reset_count.reshape(pages_local, page_len),
        jnp.zeros((local_heads, head_dim, head_dim), jnp.float32),
        jnp.zeros((), jnp.int32),
    )
    device_decay = jnp.where(
        reset_count[-1] == 0, jnp.exp(jnp.sum(log_decay, axis=0)), 0.0
    ).reshape(local_heads, head_dim)
    identity = (
        jnp.ones((local_heads, head_dim), jnp.float32),
        jnp.zeros((local_heads, head_dim, head_dim), jnp.float32),
    )
    entering = entering_2((device_decay, local_state), "ctx", compose_states, identity)[1]
    cum_device = jnp.cumsum(log_decay, axis=0).reshape(tok_count, local_heads, head_dim)
    scaled_queries = queries.reshape(tok_count, local_heads, head_dim) * jnp.exp(cum_device)
    correction = jnp.einsum(
        "thd,hde->the", scaled_queries, entering, precision=lax.Precision.HIGHEST
    )
    mixed = local_out.reshape(tok_count, local_heads, head_dim) + jnp.where(
        (reset_count == 0)[:, None, None], correction, 0.0
    )
    head_normed = (
        (mixed * lax.rsqrt(jnp.mean(mixed * mixed, axis=-1, keepdims=True) + norm_eps))
        .reshape(tok_count, head_cols)
        .astype(jnp.bfloat16)
    )
    half_rows = tok_count // rep_count
    col_block = model_width // mp_count
    attn_term = lax.dot_general(
        head_normed, w_output_t, (((1,), (1,)), ((), ())), preferred_element_type=jnp.float32
    )
    attn_all = lax.psum(attn_term.astype(jnp.bfloat16), ("mp", "rep")).astype(jnp.float32)
    residual = lax.dynamic_slice_in_dim(ordered, rep_index * half_rows, half_rows, 0).astype(
        jnp.float32
    ) + lax.dynamic_slice_in_dim(attn_all, rep_index * half_rows, half_rows, 0)
    feed_in = rms_scale(residual, feed_gain).astype(jnp.bfloat16)
    gated = jnp.einsum(
        "td,dcf->tcf", feed_in, feed_weights[:, :2], preferred_element_type=jnp.float32
    )
    hidden = (jax.nn.silu(gated[:, 0]) * gated[:, 1]).astype(jnp.bfloat16)
    down_term = lax.dot_general(
        hidden, feed_weights[:, 2], (((1,), (1,)), ((), ())), preferred_element_type=jnp.float32
    )
    summed = lax.psum_scatter(
        down_term.astype(jnp.bfloat16), "mp", scatter_dimension=1, tiled=True
    ).astype(jnp.float32)
    summed = summed + lax.dynamic_slice_in_dim(residual, mp_index * col_block, col_block, 1)
    live_half = lax.dynamic_slice_in_dim(live_tokens, rep_index * half_rows, half_rows, 0)
    return jnp.where(live_half[:, None] == 1, summed, 0.0).astype(jnp.bfloat16)


def solution(mesh):
    in_specs = (
        P("ctx", None, None),
        P("ctx"),
        P("ctx"),
        P(),
        P(("mp", "rep")),
        P(),
        P(),
        P(None, ("ctx", "mp"), None),
        P(None, ("ctx", "mp")),
        P(None, ("ctx", "mp"), None),
        P(None, ("ctx", "mp")),
    )
    out_specs = P(("ctx", "rep"), "mp")
    return jax.shard_map(shards, mesh=mesh, in_specs=in_specs, out_specs=out_specs, check_vma=False)
```

profile of v0, /device:TPU:1, one launch (start us, length us, event | category | flops | bytes accessed | tf_op | source)
XLA Modules:
  0.0 575.1 jit_solution(12584117254873081062)
XLA Ops:
  6.5 1.4 reshape.427
  8.4 1.0 reshape.429
  11.2 1.2 convert.27
  12.5 22.0 %all_to_all.15 = bf16[32,4,5248]{2,0,1:T(8,128)(2,1)} all-to-all(bf16[32,4,5248]{2,0,1:T(8,128)(2,1)S(1)} %pad_maximum_fusion), channel_id=1, replica_groups=mesh['ctx'=16,'mp'=4,'rep'=2] {'mp'}, dimensions={1} | all-to-all | bytes 2686976 | tf_op jit(solution)/shard_map/all_to_all | solution.py:140
  36.3 1.3 dynamic-update-slice
  37.6 13.0 %all-reduce = s32[16]{0:T(128)S(1)} all-reduce(s32[16]{0:T(128)S(1)} %dynamic-update-slice), channel_id=1, replica_groups=mesh['ctx'=16,'mp'=4,'rep'=2] {'ctx'}, use_global_device_ids=true, to_apply=%add | all-reduce | flops 16 | bytes 128
  50.7 18.5 %while.42 = (s32[]{:T(128)}, s32[]{:T(128)}, s32[]{:T(128)}, s32[16]{0:T(128)S(1)}, s32[]{:T(128)}) while((s32[]{:T(128)}, s32[]{:T(128)}, s32[]{:T(128)}, s32[16]{0:T(128)S(1)}, s32[]{:T(128)}) %tuple.96), condition=%wide.region_3.4_spmd, body=%wide.region_2.3_spmd.sunk | while | flops 5 | bytes 107 | solution.py:22
  69.8 5.1 gather_fusion
  75.1 3.6 fusion.21
  78.7 3.3 fusion.23
  82.0 68.7 %all-gather.4.cloned.1.call-done = bf16[2048,5248]{1,0:T(8,128)(2,1)} async-done(((bf16[128,5248]{1,0:T(8,128)(2,1)}), bf16[2048,5248]{1,0:T(8,128)(2,1)}) %all-gather.4.cloned.1.call-update) | async-done | bytes 21495824 | tf_op jit(solution)/shard_map/all_gather | solution.py:142
  150.8 2.1 slice_bitcast_fusion.3
  152.9 3.0 copy.104
  155.8 6.2 %fusion.62 = f32[1024,3,256]{2,0,1:T(8,128)S(1)} fusion(bf16[1024,2048,1]{1,0,2:T(8,128)(2,1)} %bitcast.193, bf16[3,256,2048]{2,1,0:T(8,128)(2,1)} %bitcast.197), kind=kOutput, calls=%fused_computation.127 | convolution fusion | flops 3221225472 | bytes 10485760 | tf_op jit(solution)/shard_map/dot_general | solution.py:163
  162.1 1.7 copy-done.2
  163.7 1.7 fusion.60
  165.4 1.7 div.45
  167.1 1.5 squeeze.62
  168.6 3.3 divide_multiply_fusion
  171.9 2.8 reshape_squeeze.3
  174.7 2.4 subtract_multiply_fusion
  177.1 95.7 %while.43 = (s32[]{:T(128)}, f32[2,128,128]{2,1,0:T(8,128)S(1)}, s32[]{:T(128)}, f32[8,128,2,128]{1,0,3,2:T(8,128)}, s32[8,128]{1,0:T(8,128)S(1)}, /*index=5*/f3...) while((s32[]{:T(128)}, f32[2,128,128]{2,1,0:T(8,128)S(1)}, ...), condition=%wide.region_11.12_spmd.clone, body=%wide.region_9.11_spmd.clone.sunk | while | flops 205996416 | bytes 3712938 | solution.py:84
  178.4 1.0 fusion.88
  179.4 1.2 bitcast_multiply_fusion.5
  182.7 4.8 dynamic_update_slice.6
  190.3 1.0 fusion.88
  191.4 1.2 bitcast_multiply_fusion.5
  194.7 4.8 dynamic_update_slice.6
  202.3 1.0 fusion.88
  203.4 1.2 bitcast_multiply_fusion.5
  206.6 4.8 dynamic_update_slice.6
  214.3 1.0 fusion.88
  215.3 1.2 bitcast_multiply_fusion.5
  218.6 4.8 dynamic_update_slice.6
  226.3 1.0 fusion.88
  227.3 1.2 bitcast_multiply_fusion.5
  230.6 4.8 dynamic_update_slice.6
  238.2 1.0 fusion.88
  239.3 1.2 bitcast_multiply_fusion.5
  242.5 4.8 dynamic_update_slice.6
  250.2 1.0 fusion.88
  251.2 1.2 bitcast_multiply_fusion.5
  254.5 4.8 dynamic_update_slice.6
  262.2 1.0 fusion.88
  263.2 1.2 bitcast_multiply_fusion.5
  266.5 4.8 dynamic_update_slice.6
  275.5 2.4 reshape.434
  277.9 1.7 fusion.58
  280.8 1.4 copy.111
  282.2 18.9 %all_gather.22 = bf16[16,2,128]{2,1,0:T(2,128)(2,1)S(1)} all-gather(bf16[1,2,128]{2,1,0:T(2,128)(2,1)S(1)} %fusion.52), channel_id=1, replica_groups=mesh['ctx'=16,'mp'=4,'rep'=2] {'ctx'}, dimensions={0}, use_global_device_ids=true | all-gather | bytes 8704 | tf_op jit(solution)/shard_map/all_gather | solution.py:28
  301.1 6.1 %all-gather.6.cloned.1.call-done = bf16[32,128,128]{2,1,0:T(8,128)(2,1)} async-done(((bf16[2,128,128]{2,1,0:T(8,128)(2,1)}), bf16[32,128,128]{2,1,0:T(8,128)(2,1)}) %all-gather.6.cloned.1.call-update) | async-done | bytes 1048592 | tf_op jit(solution)/shard_map/all_gather | solution.py:28
  307.2 16.2 %while.44 = (s32[]{:T(128)}, f32[2,128,128]{2,1,0:T(8,128)S(1)}, s32[]{:T(128)}, bf16[16,2,128]{2,1,0:T(2,128)(2,1)S(1)}, bf16[16,2,128,128]{3,2,1,0:T(8,128)(2,1)}, /*index=5*/s32[]{:T(128)}, s32[]{:T(128)}) while((s32[]{:T(128)}, f32[2,128,128]{2,1,0:T(8,128)S(1)}, s32[]{:T(128)}, bf16[16,2,128]{2,1,0:T(2,128)(2,1)S(1)}, ...), condition=%wide.region_14.15_spmd.clone, body=%wide.region_13.14_spmd.clone.sunk | while | flops 164100 | bytes 330345 | solution.py:45
  308.2 1.0 fusion.93
  309.2 1.0 fusion.93
  323.4 2.9 multiply_reduce_fusion.1
  326.4 4.5 convolution_convert_fusion
  331.2 14.2 %slice.81 = bf16[2048,4224]{1,0:T(8,128)(2,1)} slice(bf16[2048,5248]{1,0:T(8,128)(2,1)} %all-gather.4.cloned.1.call-done), slice={[0:2048], [1024:5248]} | slice | bytes 34603008 | tf_op jit(solution)/shard_map/slice | solution.py:145
  345.4 22.6 %copy.114 = bf16[2048,4224]{0,1:T(8,128)(2,1)} copy(bf16[2048,4224]{1,0:T(8,128)(2,1)} %slice.81) | data formatting | bytes 34603008 | tf_op jit(solution)/shard_map/slice | solution.py:145
  368.0 147.3 %all-reduce.3.cloned.1.call-done = bf16[1024,2048]{1,0:T(8,128)(2,1)} async-done(((bf16[1024,2048]{1,0:T(8,128)(2,1)}), bf16[1024,2048]{1,0:T(8,128)(2,1)}) %all-reduce.3.cloned.1.call-update) | async-done | bytes 4194320 | tf_op jit(solution)/shard_map/psum | solution.py:207
  515.3 3.2 multiply_reduce_fusion
  518.5 11.2 %fusion.19 = f32[512,2,1408]{2,0,1:T(8,128)S(1)} fusion(bf16[2048,3,1408]{0,2,1:T(8,128)(2,1)} %bitcast.190, f32[512,2048]{1,0:T(8,128)S(1)} %get-tuple-element.362, f32[2048]{0:T(1024)S(1)} %copy-done.9, f32[512]{0:T(512)S(1)} %add_rsqrt_fusion.2), kind=kOutput, calls=%fused_computation.36 | convolution fusion | flops 5908725760 | bytes 21506048 | tf_op jit(solution)/shard_map/td,dcf->tcf/dot_general | solution.py:212
  529.7 7.3 %fusion.25 = bf16[512,2048]{1,0:T(8,128)(2,1)} fusion(bf16[2048,3,1408]{0,2,1:T(8,128)(2,1)} %bitcast.191, f32[512,2,1408]{2,0,1:T(8,128)S(1)} %fusion.19), kind=kOutput, calls=%fused_computation.51 | convolution fusion | flops 2958163968 | bytes 13631488 | tf_op jit(solution)/shard_map/dot_general | solution.py:216
  537.2 29.1 %reduce-scatter.2.cloned.1.call-done = bf16[512,512]{1,0:T(8,128)(2,1)} async-done(((bf16[512,2048]{1,0:T(8,128)(2,1)}), bf16[512,512]{1,0:T(8,128)(2,1)}) %reduce-scatter.2.cloned.1.call-update) | async-done | bytes 524304 | tf_op jit(solution)/shard_map/reduce_scatter | solution.py:219
  566.3 2.3 select_convert_fusion
  (223 shorter events, 60.3 us)
Async XLA Ops:
  6.5 3.1 copy-start.3
  6.5 144.2 %all-gather.4.cloned.1.call-start = ((), (), s32[]{:S(2)}) async-start(), calls=%async_computation.2 | async-start | bytes 22839296 | tf_op jit(solution)/shard_map/all_gather | solution.py:142
  11.1 23.5 %copy-start.6 = (s32[8]{0:T(128)S(1)}, s32[8]{0:T(128)}, u32[]{:S(2)}) copy-start(s32[8]{0:T(128)} %param.19) | copy-start | bytes 100
  11.1 23.5 %copy-start.8 = (s32[8]{0:T(128)S(1)}, s32[8]{0:T(128)}, u32[]{:S(2)}) copy-start(s32[8]{0:T(128)} %param.18) | copy-start | bytes 100
  11.2 24.3 %copy-start.7 = (s32[32]{0:T(128)S(1)}, s32[32]{0:T(128)}, u32[]{:S(2)}) copy-start(s32[32]{0:T(128)} %param.20) | copy-start | bytes 388
  11.2 24.6 %copy-start.10 = (u32[128]{0:T(128)S(1)}, u32[128]{0:T(128)}, u32[]{:S(2)}) copy-start(u32[128]{0:T(128)} %constant.161) | copy-start | bytes 1540
  34.5 272.6 %all-gather.6.cloned.1.call-start = ((), (), s32[]{:S(2)}) async-start(), calls=%async_computation.5 | async-start | bytes 1114112 | tf_op jit(solution)/shard_map/all_gather | solution.py:28
  69.8 5.2 copy-start.4
  74.9 3.8 copy-start
  74.9 3.8 copy-start.5
  162.1 1.7 copy-start.2
  273.5 241.7 %all-reduce.3.cloned.1.call-start = ((), (), s32[]{:S(2)}) async-start(), calls=%async_computation.3 | async-start | bytes 8388608 | tf_op jit(solution)/shard_map/psum | solution.py:207
  331.0 235.3 %reduce-scatter.2.cloned.1.call-start = ((), (), s32[]{:S(2)}) async-start(), calls=%async_computation.4 | async-start | bytes 2621440 | tf_op jit(solution)/shard_map/reduce_scatter | solution.py:219
  515.3 3.2 copy-start.9
  518.5 11.2 %copy-start.1 = (f32[512,2048]{1,0:T(8,128)}, f32[512,2048]{1,0:T(8,128)S(1)}, u32[]{:S(2)}) copy-start(f32[512,2048]{1,0:T(8,128)S(1)} %get-tuple-element.362) | copy-start | bytes 12582916
Sparse Core Ops, SparseCore 0:
  34.7 116.0 all-gather.3
  273.7 33.4 all-gather.5
  331.1 184.1 all-reduce.2
  537.2 29.0 reduce-scatter.1
where the time goes:
time: 578 us; the launch traced here: 575 us
  waiting for transfers between devices  251 us (43%)
  local copies, waits for them, and re-layouts  127 us (22%)
  other arithmetic  65.4 us (11%)
  blocking collectives  54 us (9%)
  matrix products  42.7 us (7%)
  loops' own time  20.7 us (4%)
  between operations  14.2 us (2%)
    psum x1, waiting for transfers between devices, shards(): lax.psum(attn_term.astype(jnp.bfloat16), ('mp', 'rep')).astype(jnp.float32)  147 us
    all_gather x1, waiting for transfers between devices, shards(): served = lax.all_gather(arrived, 'ctx', axis=0, tiled=True)  68.7 us
    dynamic_update_slice x16, local copies, waits for them, and re-layouts, block_recurrence(): lax.scan(advance, (state_init, count_init), (queries, keys_in, values_in,...  38.8 us
    slice x2, local copies, waits for them, and re-layouts, shards(): served[:, 4 * head_cols:].reshape(model_width, 3, hidden_block)  36.8 us
    reduce_scatter x1, waiting for transfers between devices, shards(): lax.psum_scatter(down_term.astype(jnp.bfloat16), 'mp', scatter_dimension=...  29.1 us
    all_to_all x1, blocking collectives, shards(): lax.all_to_all(packed, 'mp', split_axis=1, concat_axis=0, tiled=True)  22 us
    all_gather x1, blocking collectives, entering_2(): lax.all_gather(part.astype(kind), axis)  18.9 us
    select_n x16, other arithmetic, entering_step(): return jax.tree.map(lambda a, b: jnp.where(reached, a, b), new, before)  15.5 us
  transfers between devices with their start and end apart: 4, of which 4 were waited for; matrix products, arithmetic and copies ran while one was open for 12% of the time, Pallas kernels for 0%

commit v1 on v0

v1 whole, which is shorter than its diff:
```python
import functools

import jax
import jax.numpy as jnp
from jax import lax
from jax.experimental import pallas as pl
from jax.experimental.pallas import tpu as pltpu
from jax.sharding import PartitionSpec as P

D = 2048
HEADS = 16
PAGE = 128
EPS = 1e-05
VMEM_LIMIT = 60 * 1024 * 1024
NT = (((1,), (1,)), ((), ()))
TN = (((0,), (0,)), ((), ()))
F32 = jnp.float32
BF16 = jnp.bfloat16


def remote(src, dst, ssem, rsem, **where):
    return pltpu.make_async_remote_copy(
        src_ref=src,
        dst_ref=dst,
        send_sem=ssem,
        recv_sem=rsem,
        device_id=where,
        device_id_type=pl.DeviceIdType.MESH,
    )


def dot(a, b, dims=None):
    if dims is None:
        return jnp.dot(a, b, preferred_element_type=F32)
    return lax.dot_general(a, b, dims, preferred_element_type=F32)


def ring_neighbours():
    mp = lax.axis_size("mp")
    me = lax.axis_index("mp")
    return lax.rem(me + mp - 1, mp), me, lax.rem(me + 1, mp), lax.rem(me + 2, mp)


class Ring:
    def __init__(self, view, rows, ssem, rsem, base):
        self.view, self.rows, self.half = view, rows, rows // 2
        self.ssem, self.rsem, self.base = ssem, rsem, base

    def copy(self, owner, row, count, k, to):
        ref = self.view(owner, row, count)
        return remote(
            ref, ref, self.ssem.at[self.base + k], self.rsem.at[self.base + k], mp=to
        )

    def start(self):
        left, me, right, _ = ring_neighbours()
        self.copy(me, 0, self.rows, 0, right).start()
        self.copy(me, 0, self.rows, 1, left).start()

    def relay(self):
        left, me, right, _ = ring_neighbours()
        self.copy(left, 0, self.rows, 0, right).wait_recv()
        self.copy(left, 0, self.half, 2, right).start()
        self.copy(right, 0, self.rows, 1, left).wait_recv()
        self.copy(right, self.half, self.half, 3, left).start()

    def finish(self):
        left, me, right, far = ring_neighbours()
        self.copy(far, 0, self.half, 2, right).wait_recv()
        self.copy(far, self.half, self.half, 3, left).wait_recv()
        self.copy(me, 0, self.rows, 0, right).wait_send()
        self.copy(me, 0, self.rows, 1, left).wait_send()
        self.copy(left, 0, self.half, 2, right).wait_send()
        self.copy(right, self.half, self.half, 3, left).wait_send()


def greet(peers):
    barrier = pltpu.get_barrier_semaphore()
    for where in peers:
        pl.semaphore_signal(
            barrier, inc=1, device_id=where, device_id_type=pl.DeviceIdType.MESH
        )
    pl.semaphore_wait(barrier, len(peers))


def mixer_kernel(
    n_ctx, blocks,
    rel_ref, w_hbm, x_ref, floor_ref, live_ref, upto_ref, out_ref,
    w_ref, q_ref, k_ref, v_ref, ctot_ref, cnt_ref, st_ref, dec_ref, run_ref, mix_ref,
    msg_ref, in_ref, oth_ref, w_sem, s_sem, r_sem, p_ssem, p_rsem, g_ssem, g_rsem,
):
    width = 2 * PAGE
    ctx, rep = lax.axis_index("ctx"), lax.axis_index("rep")
    left, me, right, _ = ring_neighbours()
    wcopy = pltpu.make_async_copy(w_hbm.at[:, pl.ds(0, PAGE), :], w_ref, w_sem)
    wcopy.start()
    peers = [dict(ctx=lax.rem(ctx + o, n_ctx)) for o in range(1, n_ctx)]
    greet(peers + [dict(mp=left), dict(mp=right), dict(rep=1 - rep)])

    upto = upto_ref[...]
    count = jnp.zeros(upto.shape, F32)
    for j in range(rel_ref.shape[0]):
        start = rel_ref[j]
        count = count + jnp.where((start >= 0) & (start < upto), 1.0, 0.0)
    cnt_ref[pl.ds(0, 1), :] = jnp.zeros((1, PAGE), F32)
    for b in range(blocks):
        cnt_ref[pl.ds(b + 1, 1), :] = count[b : b + 1, :]
    run_ref[...] = jnp.zeros_like(run_ref)
    dec_ref[...] = jnp.ones_like(dec_ref)
    row = lax.broadcasted_iota(jnp.int32, (PAGE, PAGE), 0)
    col = lax.broadcasted_iota(jnp.int32, (PAGE, PAGE), 1)
    lower = row >= col
    tri = jnp.where(lower, 1.0, 0.0).astype(BF16)
    tri = jnp.concatenate([tri, tri], axis=1)
    floor = floor_ref[...]
    wcopy.wait()

    def wide(b):
        return jnp.broadcast_to(cnt_ref[pl.ds(b + 1, 1), :], (PAGE, PAGE))

    def ends(b):
        return cnt_ref[pl.ds(b, 1), :][:, PAGE - 1 :], cnt_ref[pl.ds(b + 1, 1), :][:, PAGE - 1 :]

    def project(i, _):
        rows = pl.ds(pl.multiple_of(i * 256, 256), 256)
        x = x_ref[rows, :]
        w = w_ref[...].reshape(D, 3 * width)
        p = dot(x, w)
        pq, pf, pv = p[:, :width], p[:, width : 2 * width], p[:, 2 * width :]
        q = pq / (1.0 + jnp.exp(-pq))
        forget = floor + (1.0 - floor) / (1.0 + jnp.exp(-pf))
        logd, key = jnp.log(forget), 1.0 - forget
        v_ref[rows, :] = pv.astype(BF16)
        for half in range(2):
            b = 2 * i + half
            part = slice(half * PAGE, (half + 1) * PAGE)
            here = pl.ds(pl.multiple_of(b * PAGE, PAGE), PAGE)
            live = live_ref[pl.ds(b, 1), :]
            live = jnp.concatenate([live, live], axis=1)
            lg, kk = logd[part] * live, key[part] * live
            hi = lg.astype(BF16)
            lo = (lg - hi.astype(F32)).astype(BF16)
            c = dot(tri, jnp.concatenate([hi, lo], axis=0))
            final = c[PAGE - 1 :, :]
            before, last = ends(b)
            keep = jnp.where(wide(b).T == last, 1.0, 0.0)
            keep = jnp.concatenate([keep, keep], axis=1)
            same = jnp.where(before == last, 1.0, 0.0)
            decay = jnp.exp(final) * same
            q_ref[here, :] = (q[part] * jnp.exp(c)).astype(BF16)
            k_ref[here, :] = (kk * jnp.exp(-c)).astype(BF16)
            ke = (kk * jnp.exp(final - c) * keep).astype(BF16)
            dec = dec_ref[...]
            ctot_ref[pl.ds(b, 1), :] = dec
            dec_ref[...] = dec * decay
            for h in range(2):
                lanes = slice(h * PAGE, (h + 1) * PAGE)
                state = run_ref[h]
                st_ref[b, h] = state
                add = dot(v_ref[here, lanes], ke[:, lanes], TN)
                run_ref[h] = state * decay[:, lanes] + add
        return 0

    lax.fori_loop(0, blocks // 2, project, 0)

    dec = dec_ref[...]
    for h in range(2):
        lanes = slice(h * PAGE, (h + 1) * PAGE)
        msg_ref[h, pl.ds(0, PAGE), :] = run_ref[h].astype(BF16)
        hi = dec[:, lanes].astype(BF16)
        lo = (dec[:, lanes] - hi.astype(F32)).astype(BF16)
        first = lax.broadcasted_iota(jnp.int32, (16, PAGE), 0)
        both = jnp.where(first == 0, hi.astype(F32), jnp.where(first == 1, lo.astype(F32), 0.0))
        msg_ref[h, pl.ds(PAGE, 16), :] = both.astype(BF16)

    def state_copy(o):
        return remote(
            msg_ref, in_ref.at[o - 1], s_sem.at[o - 1], r_sem.at[o - 1],
            ctx=lax.rem(ctx + o, n_ctx),
        )

    for o in range(1, n_ctx):
        state_copy(o).start()

    def within(b, _):
        here = pl.ds(pl.multiple_of(b * PAGE, PAGE), PAGE)
        rowwise = wide(b)
        allowed = lower & (rowwise.T == rowwise)
        for h in range(2):
            lanes = slice(h * PAGE, (h + 1) * PAGE)
            scores = dot(q_ref[here, lanes], k_ref[here, lanes], NT)
            scores = jnp.where(allowed, scores, 0.0).astype(BF16)
            mix_ref[here, lanes] = dot(scores, v_ref[here, lanes])
        return 0

    lax.fori_loop(0, blocks, within, 0)

    for o in range(1, n_ctx):
        state_copy(o).wait_recv()
    run_ref[...] = jnp.zeros_like(run_ref)

    def fold(i, _):
        o = n_ctx - 1 - i
        ahead = jnp.where(o <= ctx, 1.0, 0.0)
        for h in range(2):
            tail = in_ref[o - 1, h, pl.ds(PAGE, 16), :].astype(F32)
            decay = tail[0:1, :] + tail[1:2, :]
            state = run_ref[h]
            longer = state * decay + in_ref[o - 1, h, pl.ds(0, PAGE), :].astype(F32)
            run_ref[h] = state + ahead * (longer - state)
        return 0

    lax.fori_loop(0, n_ctx - 1, fold, 0)

    def outputs(b, dst, dst_row, dst_lane):
        here = pl.ds(pl.multiple_of(b * PAGE, PAGE), PAGE)
        before, _ = ends(b)
        open_rows = wide(b).T == before
        total = ctot_ref[pl.ds(b, 1), :]
        for h in range(2):
            lanes = slice(h * PAGE, (h + 1) * PAGE)
            state = st_ref[b, h] + total[:, lanes] * run_ref[h]
            old = dot(q_ref[here, lanes], state.astype(BF16), NT)
            mixed = mix_ref[here, lanes] + jnp.where(open_rows, old, 0.0)
            scale = lax.rsqrt(jnp.mean(mixed * mixed, axis=-1, keepdims=True) + EPS)
            dst[dst_row, pl.ds(dst_lane + h * PAGE, PAGE)] = (mixed * scale).astype(BF16)

    per_half = blocks // 2

    def other_half(j, _):
        outputs((1 - rep) * per_half + j, oth_ref, pl.ds(pl.multiple_of(j * PAGE, PAGE), PAGE), 0)
        return 0

    lax.fori_loop(0, per_half, other_half, 0)

    def lane_of(owner, which):
        return pl.multiple_of((owner * 2 + which) * width, width)

    swap = remote(
        oth_ref, out_ref.at[:, pl.ds(lane_of(me, rep), width)], p_ssem, p_rsem, rep=1 - rep
    )
    swap.start()
    mine = lane_of(me, rep)

    def own_half(j, _):
        outputs(rep * per_half + j, out_ref, pl.ds(pl.multiple_of(j * PAGE, PAGE), PAGE), mine)
        return 0

    lax.fori_loop(0, per_half, own_half, 0)

    def view(which):
        return lambda owner, r, n: out_ref.at[pl.ds(r, n), pl.ds(lane_of(owner, which), width)]

    half_rows = per_half * PAGE
    ring_a = Ring(view(rep), half_rows, g_ssem, g_rsem, 0)
    ring_b = Ring(view(1 - rep), half_rows, g_ssem, g_rsem, 4)
    ring_a.start()
    swap.wait_recv()
    ring_b.start()
    ring_a.relay()
    ring_b.relay()
    ring_a.finish()
    ring_b.finish()
    swap.wait_send()
    for o in range(1, n_ctx):
        state_copy(o).wait_send()


def out_kernel(
    head_ref, wo_ref, ord_ref, gain_ref, x_ref, ss_ref, res_ref, x_ssem, x_rsem, q_ssem, q_rsem
):
    left, me, right, _ = ring_neighbours()
    greet([dict(mp=left), dict(mp=right)])
    rows = head_ref.shape[0]
    res = ord_ref[...].astype(F32) + dot(head_ref[...], wo_ref[...], NT)
    res_ref[...] = res
    x_ref[me] = (res * gain_ref[...]).astype(BF16)
    ring = Ring(lambda owner, r, n: x_ref.at[owner, pl.ds(r, n), :], rows, x_ssem, x_rsem, 0)
    ring.start()
    sq = res * res
    hi = sq.astype(BF16)
    lo = (sq - hi.astype(F32)).astype(BF16)
    ones = jnp.ones((8, sq.shape[1]), BF16)
    ss_ref[me] = dot(ones, hi, NT) + dot(ones, lo, NT)
    _, _, _, far = ring_neighbours()

    def ss_copy(k, to):
        return remote(ss_ref.at[me], ss_ref.at[me], q_ssem.at[k], q_rsem.at[k], mp=to)

    def ss_wait(k, owner, to):
        return remote(ss_ref.at[owner], ss_ref.at[owner], q_ssem.at[k], q_rsem.at[k], mp=to)

    ss_copy(0, right).start()
    ss_copy(1, left).start()
    ring.relay()
    ss_wait(0, left, right).wait_recv()
    ss_wait(2, left, right).start()
    ss_wait(1, right, left).wait_recv()
    ring.finish()
    ss_wait(2, far, right).wait_recv()
    ss_copy(0, right).wait_send()
    ss_copy(1, left).wait_send()
    ss_wait(2, left, right).wait_send()


def ffn_kernel(
    hidden_cols, live_ref, ffn_hbm, x_ref, ss_ref, res_ref, out_ref,
    wg_ref, wd_ref, hid_ref, rs_ref, part_ref, send_ref, in_ref, w_sem, s_ssem, s_rsem,
):
    left, me, right, far = ring_neighbours()
    n_mp = ffn_hbm.shape[1]
    tiles = hidden_cols // PAGE
    rows = x_ref.shape[1]
    half = rows // 2
    per = ffn_hbm.shape[0] // n_mp
    copies = []
    for y in range(n_mp):
        copies.append(
            pltpu.make_async_copy(
                ffn_hbm.at[:, y, :, pl.ds(0, 2 * hidden_cols)], wg_ref.at[y], w_sem.at[y]
            )
        )
    copies.append(
        pltpu.make_async_copy(
            ffn_hbm.at[:, :, :, pl.ds(2 * hidden_cols, hidden_cols)], wd_ref, w_sem.at[n_mp]
        )
    )
    for c in copies:
        c.start()
    greet([dict(mp=left), dict(mp=right)])
    ss = ss_ref[0]
    for y in range(1, n_mp):
        ss = ss + ss_ref[y]
    scale = lax.rsqrt(ss / D + EPS)[0:1, :]
    rs_ref[...] = jnp.broadcast_to(scale, (PAGE, rows)).T
    for c in copies[:n_mp]:
        c.wait()

    def tile(j, _):
        lanes = pl.ds(pl.multiple_of(j * 256, 256), 256)
        acc = None
        for y in range(n_mp):
            w = wg_ref[y, :, :, lanes].reshape(D // n_mp, 256)
            term = dot(x_ref[y], w)
            acc = term if acc is None else acc + term
        rs = rs_ref[...]
        g, u = acc[:, :PAGE] * rs, acc[:, PAGE:] * rs
        hid_ref[:, pl.ds(pl.multiple_of(j * PAGE, PAGE), PAGE)] = (
            g / (1.0 + jnp.exp(-g)) * u
        ).astype(BF16)
        return 0

    lax.fori_loop(0, tiles, tile, 0)
    copies[n_mp].wait()

    def partial(owner):
        first = pl.ds(owner * per, per)
        w = wd_ref[first, :, :, :]
        for y in range(n_mp):
            wy = w[:, y].reshape(per * w.shape[2], hidden_cols)
            part_ref[:, pl.ds(y * PAGE, PAGE)] = dot(hid_ref[...], wy, NT)
        mine = pl.ds(pl.multiple_of(me * PAGE, PAGE), PAGE)
        theirs = pl.ds(pl.multiple_of(owner * PAGE, PAGE), PAGE)
        part_ref[:, mine] = part_ref[:, mine] + res_ref[:, theirs]

    def hop(slot, r, n, k, to):
        return remote(
            send_ref.at[slot, pl.ds(r, n), :], in_ref.at[k, pl.ds(r, n), :],
            s_ssem.at[k], s_rsem.at[k], mp=to,
        )

    far_r = hop(0, 0, half, 0, right)
    far_l = hop(0, half, half, 1, left)
    partial(far)
    send_ref[0] = part_ref[...].astype(BF16)
    far_r.start()
    far_l.start()
    near_r = hop(1, 0, rows, 2, right)
    near_l = hop(2, 0, rows, 3, left)
    partial(right)
    far_r.wait_recv()
    send_ref[1, pl.ds(0, half), :] = (
        part_ref[pl.ds(0, half), :] + in_ref[0, pl.ds(0, half), :].astype(F32)
    ).astype(BF16)
    send_ref[1, pl.ds(half, half), :] = part_ref[pl.ds(half, half), :].astype(BF16)
    near_r.start()
    partial(left)
    far_l.wait_recv()
    send_ref[2, pl.ds(half, half), :] = (
        part_ref[pl.ds(half, half), :] + in_ref[1, pl.ds(half, half), :].astype(F32)
    ).astype(BF16)
    send_ref[2, pl.ds(0, half), :] = part_ref[pl.ds(0, half), :].astype(BF16)
    near_l.start()
    partial(me)
    near_r.wait_recv()
    near_l.wait_recv()
    for p in range(rows // PAGE):
        r = pl.ds(p * PAGE, PAGE)
        total = part_ref[r, :] + in_ref[2, r, :].astype(F32) + in_ref[3, r, :].astype(F32)
        out_ref[r, :] = jnp.where(live_ref[p] == 1, total, 0.0).astype(BF16)
    far_r.wait_send()
    far_l.wait_send()
    near_r.wait_send()
    near_l.wait_send()


VM = pl.BlockSpec(memory_space=pltpu.VMEM)
SM = pl.BlockSpec(memory_space=pltpu.SMEM)
HB = pl.BlockSpec(memory_space=pl.ANY)


def params(cid):
    return pltpu.CompilerParams(
        collective_id=cid, has_side_effects=True, vmem_limit_bytes=VMEM_LIMIT
    )


def shards(
    token_pages, page_table, live_flags, lengths, decay_floor, mixer_gain, feed_gain,
    trainer_mixer_in, trainer_mixer_out, trainer_gate_up, trainer_down,
):
    n_mp, n_rep, n_ctx = lax.axis_size("mp"), lax.axis_size("rep"), lax.axis_size("ctx")
    m, r, ctx = lax.axis_index("mp"), lax.axis_index("rep"), lax.axis_index("ctx")
    pages, page, _ = token_pages.shape
    tokens = pages * page
    half = tokens // n_rep
    wl = trainer_mixer_in.shape[1]
    cols = decay_floor.shape[0]
    hid = trainer_gate_up.shape[2] // n_mp
    block = D // n_mp

    mixer = lax.dynamic_index_in_dim(
        trainer_mixer_in.reshape(3, wl, n_mp, n_rep, cols), r, 3, keepdims=False
    ).astype(BF16)
    mixer = jnp.transpose(mixer, (2, 1, 0, 3)).reshape(n_mp, wl, 3 * cols)
    got = lax.all_to_all(mixer, "mp", split_axis=0, concat_axis=0, tiled=True)
    live_total = jnp.sum(live_flags)
    note = jnp.broadcast_to(live_total.astype(BF16), (16, 3 * cols))
    sent = jnp.concatenate([got.reshape(n_mp * wl, 3 * cols), note], axis=0)
    w_qfv = lax.all_gather(sent, "ctx", axis=0)

    wo = lax.all_gather(trainer_mixer_out.astype(BF16).T, "ctx", axis=0, tiled=True)

    gate_up = trainer_gate_up.astype(BF16).reshape(2, wl, n_mp, hid // PAGE, PAGE)
    gate_up = jnp.transpose(gate_up, (2, 1, 3, 0, 4)).reshape(n_mp, wl, 2 * hid)
    down = jnp.transpose(trainer_down.astype(BF16).reshape(n_mp, hid, wl), (0, 2, 1))
    feed = jnp.concatenate([gate_up, down], axis=2)
    feed, _ = lax.optimization_barrier((feed, got))
    feed = lax.all_to_all(feed, "mp", split_axis=0, concat_axis=0, tiled=True)
    ffn = lax.all_gather(feed, "ctx", axis=0)

    ordered = jnp.take(token_pages, page_table, axis=0).reshape(tokens, D)
    wide = ordered.astype(F32)
    normed = (
        wide * lax.rsqrt(jnp.mean(wide * wide, axis=-1, keepdims=True) + EPS) * mixer_gain
    ).astype(BF16)
    lane = jnp.arange(block)
    source = (lane // wl) * (wl * n_mp) + m * wl + lane % wl
    pick = (jnp.arange(D)[:, None] == source[None, :]).astype(BF16)
    ord_half = lax.dynamic_slice_in_dim(ordered, r * half, half, 0)
    ord_cols = jnp.dot(ord_half, pick, preferred_element_type=F32).astype(BF16)
    gain_cols = jnp.take(feed_gain, source).reshape(1, block)
    live_rows = jnp.broadcast_to(live_flags.astype(F32)[:, None], (pages, page))
    page_at = (jnp.cumsum(live_flags) - live_flags) * page
    upto = page_at[:, None] + live_flags[:, None] * (jnp.arange(page, dtype=jnp.int32)[None] + 1)

    counts = w_qfv[:, n_mp * wl, 0].astype(F32)
    base = jnp.sum(jnp.where(jnp.arange(n_ctx) < ctx, counts, 0.0)).astype(jnp.int32) * page
    rel = (jnp.cumsum(lengths) - lengths - base).astype(jnp.int32)

    heads = pl.pallas_call(
        functools.partial(mixer_kernel, n_ctx, pages),
        out_shape=jax.ShapeDtypeStruct((half, D), BF16),
        in_specs=[SM, HB, VM, VM, VM, VM],
        out_specs=VM,
        scratch_shapes=[
            pltpu.VMEM((n_ctx, PAGE, 3 * cols), BF16),
            pltpu.VMEM((tokens, cols), BF16),
            pltpu.VMEM((tokens, cols), BF16),
            pltpu.VMEM((tokens, cols), BF16),
            pltpu.VMEM((pages, cols), F32),
            pltpu.VMEM((16, PAGE), F32),
            pltpu.VMEM((pages, 2, PAGE, PAGE), F32),
            pltpu.VMEM((1, cols), F32),
            pltpu.VMEM((2, PAGE, PAGE), F32),
            pltpu.VMEM((tokens, cols), F32),
            pltpu.VMEM((2, PAGE + 16, PAGE), BF16),
            pltpu.VMEM((n_ctx - 1, 2, PAGE + 16, PAGE), BF16),
            pltpu.VMEM((half, cols), BF16),
            pltpu.SemaphoreType.DMA(()),
            pltpu.SemaphoreType.DMA((n_ctx - 1,)),
            pltpu.SemaphoreType.DMA((n_ctx - 1,)),
            pltpu.SemaphoreType.DMA(()),
            pltpu.SemaphoreType.DMA(()),
            pltpu.SemaphoreType.DMA((8,)),
            pltpu.SemaphoreType.DMA((8,)),
        ],
        compiler_params=params(0),
        name="mixer",
    )(rel, w_qfv, normed, decay_floor.reshape(1, cols), live_rows, upto)

    x_all, ss_all, res = pl.pallas_call(
        out_kernel,
        out_shape=(
            jax.ShapeDtypeStruct((n_mp, half, block), BF16),
            jax.ShapeDtypeStruct((n_mp, 8, half), F32),
            jax.ShapeDtypeStruct((half, block), F32),
        ),
        in_specs=[VM] * 4,
        out_specs=(VM, VM, VM),
        scratch_shapes=[
            pltpu.SemaphoreType.DMA((4,)),
            pltpu.SemaphoreType.DMA((4,)),
            pltpu.SemaphoreType.DMA((3,)),
            pltpu.SemaphoreType.DMA((3,)),
        ],
        compiler_params=params(1),
        name="out_proj",
    )(heads, wo, ord_cols, gain_cols)

    live_half = lax.dynamic_slice_in_dim(live_flags, r * (pages // n_rep), pages // n_rep, 0)
    final = pl.pallas_call(
        functools.partial(ffn_kernel, hid),
        out_shape=jax.ShapeDtypeStruct((half, block), BF16),
        in_specs=[SM, HB, VM, VM, VM],
        out_specs=VM,
        scratch_shapes=[
            pltpu.VMEM((n_mp, n_ctx, wl, 2 * hid), BF16),
            pltpu.VMEM((n_ctx, n_mp, wl, hid), BF16),
            pltpu.VMEM((half, hid), BF16),
            pltpu.VMEM((half, PAGE), F32),
            pltpu.VMEM((half, block), F32),
            pltpu.VMEM((3, half, block), BF16),
            pltpu.VMEM((4, half, block), BF16),
            pltpu.SemaphoreType.DMA((n_mp + 1,)),
            pltpu.SemaphoreType.DMA((4,)),
            pltpu.SemaphoreType.DMA((4,)),
        ],
        compiler_params=params(2),
        name="ffn",
    )(live_half, ffn, x_all, ss_all, res)
    per = n_ctx // n_mp
    at = (lane // wl % n_mp) * (per * wl) + lane // (wl * n_mp) * wl + lane % wl
    order = (lane[:, None] == at[None, :]).astype(BF16)
    return jnp.dot(final, order, preferred_element_type=F32).astype(BF16)


def solution(mesh):
    in_specs = (
        P("ctx", None, None),
        P("ctx"),
        P("ctx"),
        P(),
        P(("mp", "rep")),
        P(),
        P(),
        P(None, ("ctx", "mp"), None),
        P(None, ("ctx", "mp")),
        P(None, ("ctx", "mp"), None),
        P(None, ("ctx", "mp")),
    )
    out_specs = P(("ctx", "rep"), "mp")
    return jax.shard_map(shards, mesh=mesh, in_specs=in_specs, out_specs=out_specs, check_vma=False)
```

time: 578 us -> 252 us (0.44)
  waiting for transfers between devices: 251 us -> 55.8 us
  Pallas kernels: 0 us -> 126 us
  local copies, waits for them, and re-layouts: 127 us -> 14.8 us
  other arithmetic: 65.4 us -> 13.7 us
  matrix products: 42.7 us -> 4.43 us
  blocking collectives: 54 us -> 16.2 us
  loops' own time: 20.7 us -> 0 us
    psum x1 -> x0, waiting for transfers between devices: 147 us -> none  [shards(): lax.psum(attn_term.astype(jnp.bfloat16), ('mp', 'rep')).astype(jnp.float32)]
    pallas_call x0 -> x3, Pallas kernels: none -> 126 us  [the longest x1 61 us: shards(): pl.pallas_call(functools.partial(mixer_kernel, n_ctx, pages), out_shape=j...]
    slice x12 -> x0, local copies, waits for them, and re-layouts: 42.5 us -> none  [the longest x2 36.8 us: shards(): served[:, 4 * head_cols:].reshape(model_width, 3, hidden_block)]
    dynamic_update_slice x16 -> x0, local copies, waits for them, and re-layouts: 38.8 us -> none  [block_recurrence(): lax.scan(advance, (state_init, count_init), (queries, keys_in, values_in,...]
    dot_general x37 -> x2, matrix products: 42.7 us -> 4.43 us  [the longest x1 2.33 us: shards(): return jnp.dot(final, order, preferred_element_type=F32).astype(BF16)]
    reduce_scatter x1 -> x0, waiting for transfers between devices: 29.1 us -> none  [shards(): lax.psum_scatter(down_term.astype(jnp.bfloat16), 'mp', scatter_dimension=...]
    all_gather x2 -> x3, waiting for transfers between devices: 74.8 us -> 53.6 us  [the longest x1 53.4 us: shards(): ffn = lax.all_gather(feed, 'ctx', axis=0)]
    another operation x3 -> x0, loops' own time: 20.7 us -> none  [the longest x1 10.5 us: block_recurrence(): lax.scan(advance, (state_init, count_init), (queries, keys_in, values_in,...]
  transfers between devices with their start and end apart: 4 -> 4, of which waited for: 4 -> 3; matrix products, arithmetic and copies ran while one was open for 12% -> 11% of each run, Pallas kernels for 0% -> 35%
where the time goes in v1:
time: 252 us; the launch traced here: 251 us
  Pallas kernels  126 us (50%)
  waiting for transfers between devices  55.8 us (22%)
  blocking collectives  16.2 us (6%)
  local copies, waits for them, and re-layouts  14.8 us (6%)
  between operations  14.7 us (6%)
  other arithmetic  13.7 us (5%)
  starting transfers between devices  5.1 us (2%)
  matrix products  4.43 us (2%)
    pallas_call x1, Pallas kernels, shards(): pl.pallas_call(functools.partial(mixer_kernel, n_ctx, pages), out_shape=j...  61 us
    all_gather x1, waiting for transfers between devices, shards(): ffn = lax.all_gather(feed, 'ctx', axis=0)  53.4 us
    pallas_call x1, Pallas kernels, shards(): pl.pallas_call(functools.partial(ffn_kernel, hid), out_shape=jax.ShapeDty...  39 us
    pallas_call x1, Pallas kernels, shards(): pl.pallas_call(out_kernel, out_shape=(jax.ShapeDtypeStruct((n_mp, half, b...  25.8 us
    all_to_all x1, blocking collectives, shards(): feed = lax.all_to_all(feed, 'mp', split_axis=0, concat_axis=0, tiled=True)  16.2 us
    gather x1, local copies, waits for them, and re-layouts, shards(): ordered = jnp.take(token_pages, page_table, axis=0).reshape(tokens, D)  5.06 us
  transfers between devices with their start and end apart: 4, of which 3 were waited for; matrix products, arithmetic and copies ran while one was open for 11% of the time, Pallas kernels for 35%

profile of v1, /device:TPU:1, one launch (start us, length us, event | category | flops | bytes accessed | tf_op | source)
XLA Modules:
  0.0 250.5 jit_solution(7443513146049633998)
XLA Ops:
  6.5 0.0 copy-start
  6.5 0.0 copy-start.4
  6.5 0.0 copy-start.2
  6.5 1.4 reshape.302
  7.9 0.4 dynamic-slice_convert_fusion
  8.4 0.1 copy.37
  8.4 0.7 copy.33
  9.1 5.0 %all-to-all-start = ((bf16[4,32,768]{2,1,0:T(8,128)(2,1)}), bf16[4,32,768]{2,1,0:T(8,128)(2,1)S(1)}, u32[]{:S(2)}, u32[]{:S(2)}) async-start(bf16[4,32,768]{2,1,0:T(8,128)(2,1)} %bitcast.21), calls=%async_computation | async-start | bytes 393216 | tf_op jit(solution)/shard_map/all_to_all | solution.py:436
  14.1 0.0 copy-start.3
  14.1 0.0 all-gather.10.cloned.1.call-start
  14.1 0.9 reduce-window.19
  15.0 1.4 fusion.32
  17.1 2.2 all-to-all-done
  19.3 0.7 concatenate.7
  20.0 0.0 all-gather.10.cloned.1.call-update
  20.0 0.0 all-gather.6.cloned.1.call-start
  20.1 0.0 copy-done.4
  20.1 0.7 convert_bitcast_fusion
  20.8 0.0 all-gather.6.cloned.1.call-update
  20.8 0.0 all-gather.8.cloned.1.call-start
  20.8 0.0 copy-done.2
  20.8 0.1 convert_element_type.47
  20.9 0.5 reshape.299
  21.4 1.1 copy.27
  22.5 0.0 copy-start.6
  22.5 0.0 copy-start.7
  22.5 0.3 reshape.300
  22.8 0.0 copy-done.3
  22.9 0.1 pad_maximum_fusion
  23.0 16.2 %all_to_all.10 = bf16[4,32,4224]{2,1,0:T(8,128)(2,1)} all-to-all(bf16[4,32,4224]{2,1,0:T(8,128)(2,1)S(1)} %pad_maximum_fusion), channel_id=1, replica_groups=mesh['ctx'=16,'mp'=4,'rep'=2] {'mp'}, dimensions={0} | all-to-all | bytes 2162688 | tf_op jit(solution)/shard_map/all_to_all | solution.py:449
  39.3 0.0 all-gather.8.cloned.1.call-update
  39.3 0.0 copy-done.6
  39.3 0.1 copy.31
  39.4 0.1 reduce-window.18
  39.4 0.1 reduce.1
  39.6 0.0 copy-done.7
  39.6 0.6 dynamic_slice.10.live_ref
  40.2 0.0 copy-start.8
  40.2 5.1 %gather_fusion = bf16[8,128,2048]{2,1,0:T(8,128)(2,1)} fusion(bf16[8,128,2048]{2,1,0:T(8,128)(2,1)} %param.11, s32[1024]{0:T(1024)S(1)} %pad_clamp_fusion.1), kind=kCustom, calls=%fused_computation | custom fusion | bytes 8388640 | tf_op jit(solution)/shard_map/jit(_take)/gather | solution.py:452
  45.2 0.0 copy-start.5
  45.3 0.0 copy-done
  45.3 3.1 %gather_fusion.1 = f32[512]{0:T(512)S(1)} fusion(f32[2048]{0:T(1024)S(1)} %copy-done, s32[1024]{0:T(1024)S(1)} %pad_clamp_fusion), kind=kCustom, calls=%fused_computation.1 | custom fusion | bytes 6144 | tf_op jit(solution)/shard_map/jit(_take)/gather | solution.py:462
  48.4 0.0 copy-start.1
  48.5 0.0 copy-done.8
  48.5 0.1 broadcast_bitcast_fusion
  48.6 0.6 and_select_fusion.2.gain_ref
  49.2 0.7 multiply_add_fusion.upto_ref
  49.8 3.5 %multiply_reduce_fusion = f32[8,128]{1,0:T(8,128)S(1)} fusion(bf16[8,128,2048]{2,1,0:T(8,128)(2,1)} %gather_fusion, pred[8]{0:T(512)(128)(4,1)S(1)} %compare_and_fusion), kind=kLoop, calls=%fused_computation.3 | loop fusion | flops 8387584 | bytes 4198408 | tf_op jit(solution)/shard_map/reduce_sum | solution.py:455
  53.3 0.0 copy-done.5
  53.4 0.0 copy-done.1
  53.4 3.4 %multiply_convert_fusion = (bf16[1024,2048]{1,0:T(8,128)(2,1)}, bf16[1024,2048]{1,0:T(8,128)(2,1)S(1)}) fusion(f32[2048]{0:T(1024)S(1)} %copy-done.5, f32[1024]{0:T(1024)S(1)} %rsqrt_bitcast_fusion, bf16[8,128,2048]{2,1,0:T(8,128)(2,1)S(1)} %copy-done.1, pred[1024]{0:T(1024)(128)(4,1)S(1)} %broadcast_bitcast_fusion), kind=kLoop, calls=%fused_computation.2 | loop fusion | flops 10485760 | bytes 12596224 | tf_op jit(solution)/shard_map/convert_element_type | solution.py:456
  56.8 2.1 fusion.3.ord_ref
  58.9 0.2 all-gather.10.cloned.1.call-done
  59.0 1.0 fusion.7
  60.0 0.6 fusion.31
  61.3 0.5 subtract_subtract_fusion.rel_ref
  61.8 0.7 broadcast_in_dim.54.live_ref
  62.5 61.0 %mixer.1.head_ref = bf16[512,2048]{1,0:T(8,128)(2,1)} custom-call(s32[32]{0:T(128)} %subtract_subtract_fusion.rel_ref, bf16[16,144,768]{2,1,0:T(8,128)(2,1)} %bitcast.40, bf16[1024,2048]{1,0:T(8,128)(2,1)} %get-tuple-element.13.x_ref, f32[1,256]{1,0:T(1,128)} %bitcast.49, f32[8,128]{1,0:T(8,128)} %broadcast_in_dim.54.live_ref, ...), custom_call_target="tpu_custom_call" | custom-call | tf_op jit(solution)/shard_map/mixer/pallas_call | solution.py:471
  123.4 0.0 all-gather.6.cloned.1.call-done.wo_ref
  123.5 25.8 %out_proj.1 = (bf16[4,512,512]{2,1,0:T(8,128)(2,1)}, f32[4,8,512]{2,1,0:T(8,128)}, f32[512,512]{1,0:T(8,128)}) custom-call(bf16[512,2048]{1,0:T(8,128)(2,1)} %mixer.1.head_ref, bf16[512,2048]{1,0:T(8,128)(2,1)} %all-gather.6.cloned.1.call-done.wo_ref, bf16[512,512]{1,0:T(8,128)(2,1)} %fusion.3.ord_ref, f32[1,512]{1,0:T(1,128)} %and_select_fusion.2.gain_ref), custom_call_target="tpu_custom_call" | custom-call | tf_op jit(solution)/shard_map/out_proj/pallas_call | solution.py:502
  149.3 53.4 %all-gather.8.cloned.1.call-done = bf16[64,32,4224]{2,1,0:T(8,128)(2,1)} async-done(((bf16[4,32,4224]{2,1,0:T(8,128)(2,1)}), bf16[64,32,4224]{2,1,0:T(8,128)(2,1)}) %all-gather.8.cloned.1.call-update) | async-done | bytes 17301520 | tf_op jit(solution)/shard_map/all_gather | solution.py:450
  202.6 39.0 %ffn.1 = bf16[512,512]{1,0:T(8,128)(2,1)} custom-call(s32[4]{0:T(128)} %dynamic_slice.10.live_ref, bf16[16,4,32,4224]{3,2,1,0:T(8,128)(2,1)} %bitcast.37, bf16[4,512,512]{2,1,0:T(8,128)(2,1)} %get-tuple-element.10.x_ref, f32[4,8,512]{2,1,0:T(8,128)} %get-tuple-element.11.ss_ref, f32[512,512]{1,0:T(8,128)} %get-tuple-element.12.res_ref), custom_call_target="tpu_custom_call" | custom-call | tf_op jit(solution)/shard_map/ffn/pallas_call | solution.py:522
  241.6 2.3 convolution_convert_fusion
  (10 shorter events, 0.1 us)
Async XLA Ops:
  6.5 38.7 %copy-start = (f32[2048]{0:T(1024)S(1)}, f32[2048]{0:T(1024)}, u32[]{:S(2)}) copy-start(f32[2048]{0:T(1024)} %param.17) | copy-start | bytes 24580
  6.5 13.6 %copy-start.4 = (f32[2048,32]{0,1:T(8,128)S(1)}, f32[2048,32]{0,1:T(8,128)}, u32[]{:S(2)}) copy-start(f32[2048,32]{0,1:T(8,128)} %param.19) | copy-start | bytes 786436
  6.5 14.3 %copy-start.2 = (f32[2,32,5632]{2,1,0:T(8,128)S(1)}, f32[2,32,5632]{2,1,0:T(8,128)}, u32[]{:S(2)}) copy-start(f32[2,32,5632]{2,1,0:T(8,128)} %param.20) | copy-start | bytes 4325380
  9.1 10.2 %all-to-all-start = ((bf16[4,32,768]{2,1,0:T(8,128)(2,1)}), bf16[4,32,768]{2,1,0:T(8,128)(2,1)S(1)}, u32[]{:S(2)}, u32[]{:S(2)}) async-start(bf16[4,32,768]{2,1,0:T(8,128)(2,1)} %bitcast.21), calls=%async_computation | async-start | bytes 393216 | tf_op jit(solution)/shard_map/all_to_all | solution.py:436
  14.1 8.7 %copy-start.3 = (f32[5632,32]{0,1:T(8,128)S(1)}, f32[5632,32]{0,1:T(8,128)}, u32[]{:S(2)}) copy-start(f32[5632,32]{0,1:T(8,128)} %param.21) | copy-start | bytes 2162692
  14.1 44.9 %all-gather.10.cloned.1.call-start = ((), (), s32[]{:S(2)}) async-start(), calls=%async_computation.4 | async-start | bytes 3760128 | tf_op jit(solution)/shard_map/all_gather | solution.py:440
  20.0 103.4 %all-gather.6.cloned.1.call-start = ((), (), s32[]{:S(2)}) async-start(), calls=%async_computation.2 | async-start | bytes 2228224 | tf_op jit(solution)/shard_map/all_gather | solution.py:442
  20.8 181.9 %all-gather.8.cloned.1.call-start = ((), (), s32[]{:S(2)}) async-start(), calls=%async_computation.3 | async-start | bytes 18382848 | tf_op jit(solution)/shard_map/all_gather | solution.py:450
  22.5 16.8 %copy-start.6 = (s32[32]{0:T(128)S(1)}, s32[32]{0:T(128)}, u32[]{:S(2)}) copy-start(s32[32]{0:T(128)} %param.14) | copy-start | bytes 388
  22.5 17.0 %copy-start.7 = (s32[8]{0:T(128)S(1)}, s32[8]{0:T(128)}, u32[]{:S(2)}) copy-start(s32[8]{0:T(128)} %param.13) | copy-start | bytes 100
  40.2 8.3 %copy-start.8 = (s32[8]{0:T(128)S(1)}, s32[8]{0:T(128)}, u32[]{:S(2)}) copy-start(s32[8]{0:T(128)} %param.12) | copy-start | bytes 100
  45.2 8.1 %copy-start.5 = (f32[2048]{0:T(1024)S(1)}, f32[2048]{0:T(1024)}, u32[]{:S(2)}) copy-start(f32[2048]{0:T(1024)} %param.16) | copy-start | bytes 24580
  48.4 4.9 %copy-start.1 = (bf16[8,128,2048]{2,1,0:T(8,128)(2,1)S(1)}, bf16[8,128,2048]{2,1,0:T(8,128)(2,1)}, u32[]{:S(2)}) copy-start(bf16[8,128,2048]{2,1,0:T(8,128)(2,1)} %gather_fusion) | copy-start | bytes 12582916
Sparse Core Ops, SparseCore 0:
  20.2 38.8 all-gather.9
  60.7 44.3 all-gather.5
  106.8 95.7 all-gather.7

commit v2 on v1

v2 whole, which is shorter than its diff:
```python
import functools

import jax
import jax.numpy as jnp
from jax import lax
from jax.experimental import pallas as pl
from jax.experimental.pallas import tpu as pltpu
from jax.sharding import PartitionSpec as P

D = 2048
HEADS = 16
PAGE = 128
EPS = 1e-05
VMEM_LIMIT = 60 * 1024 * 1024
NT = (((1,), (1,)), ((), ()))
TN = (((0,), (0,)), ((), ()))
F32 = jnp.float32
BF16 = jnp.bfloat16


def remote(src, dst, ssem, rsem, **where):
    return pltpu.make_async_remote_copy(
        src_ref=src,
        dst_ref=dst,
        send_sem=ssem,
        recv_sem=rsem,
        device_id=where,
        device_id_type=pl.DeviceIdType.MESH,
    )


def dot(a, b, dims=None):
    if dims is None:
        return jnp.dot(a, b, preferred_element_type=F32)
    return lax.dot_general(a, b, dims, preferred_element_type=F32)


def ring_neighbours():
    mp = lax.axis_size("mp")
    me = lax.axis_index("mp")
    return lax.rem(me + mp - 1, mp), me, lax.rem(me + 1, mp), lax.rem(me + 2, mp)


class Ring:
    def __init__(self, view, rows, ssem, rsem, base):
        self.view, self.rows, self.half = view, rows, rows // 2
        self.ssem, self.rsem, self.base = ssem, rsem, base

    def copy(self, owner, row, count, k, to):
        ref = self.view(owner, row, count)
        return remote(
            ref, ref, self.ssem.at[self.base + k], self.rsem.at[self.base + k], mp=to
        )

    def start(self):
        left, me, right, _ = ring_neighbours()
        self.copy(me, 0, self.rows, 0, right).start()
        self.copy(me, 0, self.rows, 1, left).start()

    def relay(self):
        left, me, right, _ = ring_neighbours()
        self.copy(left, 0, self.rows, 0, right).wait_recv()
        self.copy(left, 0, self.half, 2, right).start()
        self.copy(right, 0, self.rows, 1, left).wait_recv()
        self.copy(right, self.half, self.half, 3, left).start()

    def finish(self):
        left, me, right, far = ring_neighbours()
        self.copy(far, 0, self.half, 2, right).wait_recv()
        self.copy(far, self.half, self.half, 3, left).wait_recv()
        self.copy(me, 0, self.rows, 0, right).wait_send()
        self.copy(me, 0, self.rows, 1, left).wait_send()
        self.copy(left, 0, self.half, 2, right).wait_send()
        self.copy(right, self.half, self.half, 3, left).wait_send()


class Bulk:
    def __init__(self, w, pack, both, ysend, yrecv, zsend, zrecv, xsend, xrecv, csend, crecv):
        self.w, self.pack, self.both = w, pack, both
        self.ys, self.yr, self.zs, self.zr = ysend, yrecv, zsend, zrecv
        self.xs, self.xr, self.cs, self.cr = xsend, xrecv, csend, crecv
        self.started = []
        n_ctx = lax.axis_size("ctx")
        self.n_z = n_ctx // 4
        c = lax.axis_index("ctx")
        self.core, self.z, self.x = lax.rem(c, 2), lax.rem(c // 2, self.n_z), c // (2 * self.n_z)
        self.mp, self.me = lax.axis_size("mp"), lax.axis_index("mp")
        self.rep = lax.axis_index("rep")
        self.rows = w.shape[2]
        self.top, self.bottom = pl.ds(0, self.rows // 2), pl.ds(self.rows // 2, self.rows // 2)
        self.all = pl.ds(0, self.rows)

    def ctx(self, xr=0, dz=0, other=0):
        x = self.x if xr == 0 else 1 - self.x
        core = self.core if other == 0 else 1 - self.core
        return x * (2 * self.n_z) + lax.rem(self.z + dz + self.n_z, self.n_z) * 2 + core

    def owner(self, i):
        return lax.rem(self.me + self.mp - (0, 1, 3, 2)[i], self.mp) if self.pack is not None else 0

    def piece(self, i, rows, xr=0, zr=0, other=0):
        return self.w.at[self.ctx(xr, (0, -1, 1, 2)[zr], other), self.owner(i), rows, :]

    def go(self, copy):
        copy.start()
        self.started.append(copy)

    def y_copy(self, i):
        d = (0, 1, 3, 2)[i]
        to = lax.rem(self.me + d, self.mp)
        return remote(
            self.pack.at[to], self.w.at[self.ctx(), self.me], self.ys.at[i - 1], self.yr.at[i - 1],
            mp=to,
        )

    def y_start(self):
        for i in (1, 2, 3):
            self.go(self.y_copy(i))

    def z_copy(self, i, k, zr, rows):
        ref = self.piece(i, rows, 0, zr)
        to = self.ctx(0, 1 if k in (0, 2) else -1)
        return remote(ref, ref, self.zs.at[i, k], self.zr.at[i, k], ctx=to)

    def x_copies(self, i, zr, xr):
        if self.both:
            a, b = self.piece(i, self.top, xr, zr), self.piece(i, self.bottom, xr, zr)
        else:
            a, b = self.piece(i, self.all, xr, zr), None
        out = [remote(a, a, self.xs.at[i, zr, 0], self.xr.at[i, zr, 0], ctx=self.ctx(1))]
        if b is not None:
            out.append(
                remote(
                    b, b, self.xs.at[i, zr, 1], self.xr.at[i, zr, 1],
                    ctx=self.ctx(1), rep=1 - self.rep,
                )
            )
        return out

    def c_copy(self, i, xr, zr, other=0):
        ref = self.piece(i, self.all, xr, zr, other)
        return remote(
            ref, ref, self.cs.at[i, xr, zr], self.cr.at[i, xr, zr], ctx=self.ctx(0, 0, 1)
        )

    def onward(self, i, zr):
        for copy in self.x_copies(i, zr, 0):
            self.go(copy)
        self.go(self.c_copy(i, 0, zr))

    def z_start(self, i):
        if i:
            self.y_copy(i).wait_recv()
        self.go(self.z_copy(i, 0, 0, self.all))
        self.go(self.z_copy(i, 1, 0, self.all))
        self.onward(i, 0)

    def z_relay(self, i):
        self.z_copy(i, 0, 1, self.all).wait_recv()
        self.go(self.z_copy(i, 2, 1, self.top))
        self.z_copy(i, 1, 2, self.all).wait_recv()
        self.go(self.z_copy(i, 3, 2, self.bottom))
        self.onward(i, 1)
        self.onward(i, 2)

    def z_far(self, i):
        self.z_copy(i, 2, 3, self.top).wait_recv()
        self.z_copy(i, 3, 3, self.bottom).wait_recv()
        self.onward(i, 3)

    def x_take(self, i, zr):
        for copy in self.x_copies(i, zr, 1):
            copy.wait_recv()
        self.go(self.c_copy(i, 1, zr))

    def c_take(self, i):
        for xr in range(2):
            for zr in range(4):
                self.c_copy(i, xr, zr, 1).wait_recv()

    def drain(self):
        for copy in self.started:
            copy.wait_send()


def greet(peers):
    barrier = pltpu.get_barrier_semaphore()
    for where in peers:
        pl.semaphore_signal(
            barrier, inc=1, device_id=where, device_id_type=pl.DeviceIdType.MESH
        )
    pl.semaphore_wait(barrier, len(peers))


def layer_kernel(
    n_ctx, pages,
    pt_ref, live_ref, len_ref, tok_ref, floor_ref, mgain_ref, fgain_ref,
    tin_ref, tout_ref, tgu_ref, tdn_ref,
    out_ref,
    wq_ref, wo_ref, wf_ref, pkq_ref, pkf_ref, x_ref, ord_ref,
    q_ref, k_ref, v_ref, ctot_ref, cnt_ref, st_ref, dec_ref, run_ref, mix_ref,
    msg_ref, in_ref, num_ref, nin_ref, oth_ref, head_ref, xall_ref, ss_ref, res_ref,
    hid_ref, rs_ref, part_ref, send_ref, rin_ref,
    *sems,
):
    (n_ssem, n_rsem, s_sem, r_sem, p_ssem, p_rsem, g_ssem, g_rsem, a_ssem, a_rsem,
     b_ssem, b_rsem, t_ssem, t_rsem) = sems[:14]
    sq, so, sf = sems[14:22], sems[22:28], sems[28:36]
    width = 2 * PAGE
    cols, hid = width, tdn_ref.shape[1] // 4
    ctx, rep = lax.axis_index("ctx"), lax.axis_index("rep")
    left, me, right, far = ring_neighbours()
    half_pages = pages // 2
    rows = half_pages * PAGE
    wl = tin_ref.shape[1]
    bq = Bulk(wq_ref, pkq_ref, False, *sq)
    bo = Bulk(wo_ref, None, True, None, None, *so)
    bf = Bulk(wf_ref, pkf_ref, True, *sf)

    for y in range(4):
        for t in range(3):
            lane = pl.multiple_of((y * 2 + rep) * cols, cols)
            pkq_ref[y, :, pl.ds(t * cols, cols)] = tin_ref[t, :, pl.ds(lane, cols)].astype(BF16)
    wq_ref[ctx, me] = pkq_ref[me]

    peers = [dict(ctx=lax.rem(ctx + o, n_ctx)) for o in range(1, n_ctx)]
    greet(
        peers
        + [dict(mp=left), dict(mp=right), dict(mp=far), dict(rep=1 - rep)]
        + [dict(ctx=bq.ctx(1), rep=1 - rep)]
    )
    bq.y_start()
    bq.z_start(0)

    row8 = lax.broadcasted_iota(jnp.int32, (pages, PAGE), 0)
    lane8 = lax.broadcasted_iota(jnp.int32, (pages, PAGE), 1)
    upto = jnp.zeros((pages, PAGE), jnp.int32)
    alive = jnp.zeros((pages, PAGE), F32)
    so_far = jnp.int32(0)
    for b in range(pages):
        flag = live_ref[b]
        upto = jnp.where(row8 == b, so_far * PAGE + flag * (lane8 + 1), upto)
        alive = jnp.where(row8 == b, flag.astype(F32), alive)
        so_far = so_far + flag
    num_ref[...] = jnp.zeros((pages, PAGE), jnp.int32) + so_far * PAGE

    def num_copy(o):
        return remote(
            num_ref, nin_ref.at[o - 1], n_ssem.at[o - 1], n_rsem.at[o - 1],
            ctx=lax.rem(ctx + o, n_ctx),
        )

    for o in range(1, n_ctx):
        num_copy(o).start()

    wo_ref[ctx, 0] = tout_ref[...].astype(BF16)
    for y in range(4):
        for j in range(hid // PAGE):
            for t in range(2):
                pkf_ref[y, :, pl.ds(j * 2 * PAGE + t * PAGE, PAGE)] = tgu_ref[
                    t, :, pl.ds(y * hid + j * PAGE, PAGE)
                ].astype(BF16)
        pkf_ref[y, :, pl.ds(2 * hid, hid)] = tdn_ref[:, pl.ds(y * hid, hid)].astype(BF16)
    wf_ref[ctx, me] = pkf_ref[me]
    bf.y_start()

    def norm(b):
        x = tok_ref[pt_ref[b]].astype(F32)
        scale = lax.rsqrt(jnp.mean(x * x, axis=-1, keepdims=True) + EPS)
        x_ref[pl.ds(b * PAGE, PAGE), :] = (x * scale * mgain_ref[...]).astype(BF16)

    lane1 = lax.broadcasted_iota(jnp.int32, (1, PAGE), 1) // wl

    def my_columns(read, t):
        tile = None
        for k in range(4):
            turned = pltpu.roll(read(t * 4 + k), lax.rem(wl * (k + 4) - wl * me, PAGE), 1)
            tile = turned if tile is None else jnp.where(lane1 == k, turned, tile)
        return tile

    def pick(j):
        page = pt_ref[rep * half_pages + j]
        for t in range(4):
            tile = my_columns(
                lambda c: tok_ref[page, :, pl.ds(c * PAGE, PAGE)].astype(F32), t
            )
            ord_ref[pl.ds(j * PAGE, PAGE), pl.ds(t * PAGE, PAGE)] = tile

    norm(0)
    bq.z_start(1)
    bq.z_start(2)
    bo.z_start(0)
    bf.z_start(0)
    norm(1)
    norm(2)
    bq.z_start(3)
    bq.z_relay(0)
    norm(3)
    bq.z_relay(1)
    bq.z_relay(2)
    norm(4)
    norm(5)
    bq.z_relay(3)
    bq.z_far(0)
    norm(6)
    bq.z_far(1)
    bq.z_far(2)
    norm(7)
    bq.z_far(3)

    for o in range(1, n_ctx):
        num_copy(o).wait_recv()
    base = jnp.zeros((pages, PAGE), jnp.int32)
    for o in range(1, n_ctx):
        base = base + jnp.where(o <= ctx, nin_ref[o - 1], 0)
    count = jnp.zeros((pages, PAGE), F32)
    start = jnp.int32(0)
    for j in range(len_ref.shape[0]):
        count = count + jnp.where((base <= start) & (start < base + upto), 1.0, 0.0)
        start = start + len_ref[j]
    cnt_ref[pl.ds(0, 1), :] = jnp.zeros((1, PAGE), F32)
    for b in range(pages):
        cnt_ref[pl.ds(b + 1, 1), :] = count[b : b + 1, :]
    run_ref[...] = jnp.zeros_like(run_ref)
    dec_ref[...] = jnp.ones_like(dec_ref)
    row = lax.broadcasted_iota(jnp.int32, (PAGE, PAGE), 0)
    col = lax.broadcasted_iota(jnp.int32, (PAGE, PAGE), 1)
    lower = row >= col
    tri = jnp.where(lower, 1.0, 0.0).astype(BF16)
    tri = jnp.concatenate([tri, tri], axis=1)
    floor = floor_ref[...]
    for i in range(4):
        for zr in range(4):
            bq.x_take(i, zr)
    for i in range(4):
        bq.c_take(i)

    def wide(b):
        return jnp.broadcast_to(cnt_ref[pl.ds(b + 1, 1), :], (PAGE, PAGE))

    def ends(b):
        return cnt_ref[pl.ds(b, 1), :][:, PAGE - 1 :], cnt_ref[pl.ds(b + 1, 1), :][:, PAGE - 1 :]

    def project(i):
        here2 = pl.ds(i * 256, 256)
        p = dot(x_ref[here2, :], wq_ref[...].reshape(D, 3 * width))
        pq, pf, pv = p[:, :width], p[:, width : 2 * width], p[:, 2 * width :]
        q = pq / (1.0 + jnp.exp(-pq))
        forget = floor + (1.0 - floor) / (1.0 + jnp.exp(-pf))
        logd, key = jnp.log(forget), 1.0 - forget
        v_ref[here2, :] = pv.astype(BF16)
        for h2 in range(2):
            b = 2 * i + h2
            part = slice(h2 * PAGE, (h2 + 1) * PAGE)
            here = pl.ds(b * PAGE, PAGE)
            live = alive[b : b + 1, :]
            live = jnp.concatenate([live, live], axis=1)
            lg, kk = logd[part] * live, key[part] * live
            hi = lg.astype(BF16)
            lo = (lg - hi.astype(F32)).astype(BF16)
            c = dot(tri, jnp.concatenate([hi, lo], axis=0))
            final = c[PAGE - 1 :, :]
            before, last = ends(b)
            keep = jnp.where(wide(b).T == last, 1.0, 0.0)
            keep = jnp.concatenate([keep, keep], axis=1)
            same = jnp.where(before == last, 1.0, 0.0)
            decay = jnp.exp(final) * same
            q_ref[here, :] = (q[part] * jnp.exp(c)).astype(BF16)
            k_ref[here, :] = (kk * jnp.exp(-c)).astype(BF16)
            ke = (kk * jnp.exp(final - c) * keep).astype(BF16)
            dec = dec_ref[...]
            ctot_ref[pl.ds(b, 1), :] = dec
            dec_ref[...] = dec * decay
            for h in range(2):
                lanes = slice(h * PAGE, (h + 1) * PAGE)
                state = run_ref[h]
                st_ref[b, h] = state
                add = dot(v_ref[here, lanes], ke[:, lanes], TN)
                run_ref[h] = state * decay[:, lanes] + add

    project(0)
    bf.z_start(1)
    bf.z_start(2)
    project(1)
    bf.z_start(3)
    bo.z_relay(0)
    bf.z_relay(0)
    project(2)
    bo.z_far(0)
    bf.z_relay(1)
    project(3)

    dec = dec_ref[...]
    for h in range(2):
        lanes = slice(h * PAGE, (h + 1) * PAGE)
        msg_ref[h, pl.ds(0, PAGE), :] = run_ref[h].astype(BF16)
        hi = dec[:, lanes].astype(BF16)
        lo = (dec[:, lanes] - hi.astype(F32)).astype(BF16)
        first = lax.broadcasted_iota(jnp.int32, (16, PAGE), 0)
        both = jnp.where(first == 0, hi.astype(F32), jnp.where(first == 1, lo.astype(F32), 0.0))
        msg_ref[h, pl.ds(PAGE, 16), :] = both.astype(BF16)

    def state_copy(o):
        return remote(
            msg_ref, in_ref.at[o - 1], s_sem.at[o - 1], r_sem.at[o - 1],
            ctx=lax.rem(ctx + o, n_ctx),
        )

    for o in range(1, n_ctx):
        state_copy(o).start()
    bf.z_relay(2)

    def within(b, _):
        here = pl.ds(pl.multiple_of(b * PAGE, PAGE), PAGE)
        rowwise = wide(b)
        allowed = lower & (rowwise.T == rowwise)
        for h in range(2):
            lanes = slice(h * PAGE, (h + 1) * PAGE)
            scores = dot(q_ref[here, lanes], k_ref[here, lanes], NT)
            scores = jnp.where(allowed, scores, 0.0).astype(BF16)
            mix_ref[here, lanes] = dot(scores, v_ref[here, lanes])
        return 0

    lax.fori_loop(0, pages, within, 0)
    bf.z_relay(3)
    bf.z_far(0)
    for j in range(half_pages):
        pick(j)

    for o in range(1, n_ctx):
        state_copy(o).wait_recv()
    run_ref[...] = jnp.zeros_like(run_ref)

    def fold(i, _):
        o = n_ctx - 1 - i
        ahead = jnp.where(o <= ctx, 1.0, 0.0)
        for h in range(2):
            tail = in_ref[o - 1, h, pl.ds(PAGE, 16), :].astype(F32)
            decay = tail[0:1, :] + tail[1:2, :]
            state = run_ref[h]
            longer = state * decay + in_ref[o - 1, h, pl.ds(0, PAGE), :].astype(F32)
            run_ref[h] = state + ahead * (longer - state)
        return 0

    lax.fori_loop(0, n_ctx - 1, fold, 0)

    def outputs(b, dst, dst_row, dst_lane):
        here = pl.ds(pl.multiple_of(b * PAGE, PAGE), PAGE)
        before, _ = ends(b)
        open_rows = wide(b).T == before
        total = ctot_ref[pl.ds(b, 1), :]
        for h in range(2):
            lanes = slice(h * PAGE, (h + 1) * PAGE)
            state = st_ref[b, h] + total[:, lanes] * run_ref[h]
            old = dot(q_ref[here, lanes], state.astype(BF16), NT)
            mixed = mix_ref[here, lanes] + jnp.where(open_rows, old, 0.0)
            scale = lax.rsqrt(jnp.mean(mixed * mixed, axis=-1, keepdims=True) + EPS)
            dst[dst_row, pl.ds(dst_lane + h * PAGE, PAGE)] = (mixed * scale).astype(BF16)

    def other_half(j, _):
        outputs((1 - rep) * half_pages + j, oth_ref, pl.ds(pl.multiple_of(j * PAGE, PAGE), PAGE), 0)
        return 0

    lax.fori_loop(0, half_pages, other_half, 0)

    def lane_of(owner, which):
        return pl.multiple_of((owner * 2 + which) * width, width)

    swap = remote(
        oth_ref, head_ref.at[:, pl.ds(lane_of(me, rep), width)], p_ssem, p_rsem, rep=1 - rep
    )
    swap.start()
    mine = lane_of(me, rep)

    def own_half(j, _):
        outputs(rep * half_pages + j, head_ref, pl.ds(pl.multiple_of(j * PAGE, PAGE), PAGE), mine)
        return 0

    lax.fori_loop(0, half_pages, own_half, 0)

    def view(which):
        return lambda owner, r, n: head_ref.at[pl.ds(r, n), pl.ds(lane_of(owner, which), width)]

    ring_a = Ring(view(rep), rows, g_ssem, g_rsem, 0)
    ring_b = Ring(view(1 - rep), rows, g_ssem, g_rsem, 4)
    ring_a.start()
    bf.z_far(1)
    swap.wait_recv()
    ring_b.start()
    bf.z_far(2)
    ring_a.relay()
    bf.z_far(3)
    for zr in range(4):
        bo.x_take(0, zr)
    ring_b.relay()
    bo.c_take(0)
    for zr in range(4):
        bf.x_take(0, zr)
    gain = jnp.concatenate(
        [my_columns(lambda c: jnp.broadcast_to(fgain_ref[:, pl.ds(c * PAGE, PAGE)], (8, PAGE)), t)[0:1] for t in range(4)],
        axis=1,
    )
    ring_a.finish()
    ring_b.finish()

    res = ord_ref[...] + dot(head_ref[...], wo_ref[...].reshape(4 * PAGE, D), NT)
    xall_ref[me] = (res * gain).astype(BF16)
    ring = Ring(lambda owner, r, n: xall_ref.at[owner, pl.ds(r, n), :], rows, a_ssem, a_rsem, 0)
    ring.start()
    sqr = res * res
    hi = sqr.astype(BF16)
    lo = (sqr - hi.astype(F32)).astype(BF16)
    ones = jnp.ones((8, sqr.shape[1]), BF16)
    ss_ref[me] = dot(ones, hi, NT) + dot(ones, lo, NT)

    def ss_copy(k, owner, to):
        return remote(ss_ref.at[owner], ss_ref.at[owner], b_ssem.at[k], b_rsem.at[k], mp=to)

    ss_copy(0, me, right).start()
    ss_copy(1, me, left).start()
    ord_ref[...] = res
    for i in range(1, 4):
        for zr in range(4):
            bf.x_take(i, zr)
    for t in range(4):
        tile = ord_ref[:, pl.ds(t * PAGE, PAGE)]
        for k in range(4):
            turned = pltpu.roll(tile, lax.rem(wl * (4 - k) + wl * me, PAGE), 1)
            res_ref[:, pl.ds((t * 4 + k) * PAGE, PAGE)] = jnp.where(lane1 == me, turned, 0.0)
    ring.relay()
    ss_copy(0, left, right).wait_recv()
    ss_copy(2, left, right).start()
    ss_copy(1, right, left).wait_recv()
    for i in range(4):
        bf.c_take(i)
    ss_copy(2, far, right).wait_recv()
    ring.finish()

    ss = ss_ref[0]
    for y in range(1, 4):
        ss = ss + ss_ref[y]
    scale = lax.rsqrt(ss / D + EPS)[0:1, :]
    rs_ref[...] = jnp.broadcast_to(scale, (PAGE, rows)).T

    def tile(j, _):
        lanes = pl.ds(pl.multiple_of(j * 256, 256), 256)
        acc = None
        for y in range(4):
            w = wf_ref[:, y, :, lanes].reshape(D // 4, 256)
            term = dot(xall_ref[y], w)
            acc = term if acc is None else acc + term
        rs = rs_ref[...]
        g, u = acc[:, :PAGE] * rs, acc[:, PAGE:] * rs
        hid_ref[:, pl.ds(pl.multiple_of(j * PAGE, PAGE), PAGE)] = (
            g / (1.0 + jnp.exp(-g)) * u
        ).astype(BF16)
        return 0

    lax.fori_loop(0, hid // PAGE, tile, 0)

    def partial(owner):
        w = wf_ref[pl.ds(owner * 4, 4), :, :, pl.ds(2 * hid, hid)].reshape(4 * PAGE, hid)
        theirs = pl.ds(pl.multiple_of(owner * 4 * PAGE, PAGE), 4 * PAGE)
        part_ref[...] = res_ref[:, theirs] + dot(hid_ref[...], w, NT)

    half = rows // 2

    def hop(slot, r, n, k, to):
        return remote(
            send_ref.at[slot, pl.ds(r, n), :], rin_ref.at[k, pl.ds(r, n), :],
            t_ssem.at[k], t_rsem.at[k], mp=to,
        )

    far_r = hop(0, 0, half, 0, right)
    far_l = hop(0, half, half, 1, left)
    partial(far)
    send_ref[0] = part_ref[...].astype(BF16)
    far_r.start()
    far_l.start()
    near_r = hop(1, 0, rows, 2, right)
    near_l = hop(2, 0, rows, 3, left)
    upper, under = pl.ds(0, half), pl.ds(half, half)
    partial(right)
    far_r.wait_recv()
    send_ref[1, upper, :] = (part_ref[upper, :] + rin_ref[0, upper, :].astype(F32)).astype(BF16)
    send_ref[1, under, :] = part_ref[under, :].astype(BF16)
    near_r.start()
    partial(left)
    far_l.wait_recv()
    send_ref[2, under, :] = (part_ref[under, :] + rin_ref[1, under, :].astype(F32)).astype(BF16)
    send_ref[2, upper, :] = part_ref[upper, :].astype(BF16)
    near_l.start()
    partial(me)
    near_r.wait_recv()
    near_l.wait_recv()
    for p in range(half_pages):
        r = pl.ds(p * PAGE, PAGE)
        total = part_ref[r, :] + rin_ref[2, r, :].astype(F32) + rin_ref[3, r, :].astype(F32)
        out_ref[r, :] = jnp.where(live_ref[rep * half_pages + p] == 1, total, 0.0).astype(BF16)

    far_r.wait_send()
    far_l.wait_send()
    near_r.wait_send()
    near_l.wait_send()
    ss_copy(0, me, right).wait_send()
    ss_copy(1, me, left).wait_send()
    ss_copy(2, left, right).wait_send()
    swap.wait_send()
    for o in range(1, n_ctx):
        state_copy(o).wait_send()
        num_copy(o).wait_send()
    for bulk in (bq, bo, bf):
        bulk.drain()


VM = pl.BlockSpec(memory_space=pltpu.VMEM)
SM = pl.BlockSpec(memory_space=pltpu.SMEM)


def shards(
    token_pages, page_table, live_flags, lengths, decay_floor, mixer_gain, feed_gain,
    trainer_mixer_in, trainer_mixer_out, trainer_gate_up, trainer_down,
):
    n_ctx = lax.axis_size("ctx")
    pages, page, _ = token_pages.shape
    tokens, half = pages * page, pages * page // 2
    wl = trainer_mixer_in.shape[1]
    cols = decay_floor.shape[0]
    hid = trainer_gate_up.shape[2] // 4
    block = D // 4
    dma = pltpu.SemaphoreType.DMA

    def bulk_sems(n, y):
        near = [dma((3,)), dma((3,))] if y else []
        return near + [
            dma((n, 4)), dma((n, 4)), dma((n, 4, 2)), dma((n, 4, 2)), dma((n, 2, 4)), dma((n, 2, 4)),
        ]

    return pl.pallas_call(
        functools.partial(layer_kernel, n_ctx, pages),
        out_shape=jax.ShapeDtypeStruct((half, block), BF16),
        in_specs=[SM, SM, SM] + [VM] * 8,
        out_specs=VM,
        scratch_shapes=[
            pltpu.VMEM((n_ctx, 4, wl, 3 * cols), BF16),
            pltpu.VMEM((n_ctx, 1, wl, D), BF16),
            pltpu.VMEM((n_ctx, 4, wl, 3 * hid), BF16),
            pltpu.VMEM((4, wl, 3 * cols), BF16),
            pltpu.VMEM((4, wl, 3 * hid), BF16),
            pltpu.VMEM((tokens, D), BF16),
            pltpu.VMEM((half, block), F32),
            pltpu.VMEM((tokens, cols), BF16),
            pltpu.VMEM((tokens, cols), BF16),
            pltpu.VMEM((tokens, cols), BF16),
            pltpu.VMEM((pages, cols), F32),
            pltpu.VMEM((16, PAGE), F32),
            pltpu.VMEM((pages, 2, PAGE, PAGE), F32),
            pltpu.VMEM((1, cols), F32),
            pltpu.VMEM((2, PAGE, PAGE), F32),
            pltpu.VMEM((tokens, cols), F32),
            pltpu.VMEM((2, PAGE + 16, PAGE), BF16),
            pltpu.VMEM((n_ctx - 1, 2, PAGE + 16, PAGE), BF16),
            pltpu.VMEM((pages, PAGE), jnp.int32),
            pltpu.VMEM((n_ctx - 1, pages, PAGE), jnp.int32),
            pltpu.VMEM((half, cols), BF16),
            pltpu.VMEM((half, D), BF16),
            pltpu.VMEM((4, half, block), BF16),
            pltpu.VMEM((4, 8, half), F32),
            pltpu.VMEM((half, D), F32),
            pltpu.VMEM((half, hid), BF16),
            pltpu.VMEM((half, PAGE), F32),
            pltpu.VMEM((half, block), F32),
            pltpu.VMEM((3, half, block), BF16),
            pltpu.VMEM((4, half, block), BF16),
            dma((n_ctx - 1,)), dma((n_ctx - 1,)), dma((n_ctx - 1,)), dma((n_ctx - 1,)),
            dma(()), dma(()), dma((8,)), dma((8,)), dma((4,)), dma((4,)),
            dma((3,)), dma((3,)), dma((4,)), dma((4,)),
        ]
        + bulk_sems(4, True) + bulk_sems(1, False) + bulk_sems(4, True),
        compiler_params=pltpu.CompilerParams(
            collective_id=0, has_side_effects=True, vmem_limit_bytes=VMEM_LIMIT
        ),
        name="layer",
    )(
        page_table, live_flags, lengths, token_pages, decay_floor.reshape(1, cols),
        mixer_gain.reshape(1, D), feed_gain.reshape(1, D),
        trainer_mixer_in, trainer_mixer_out.T, trainer_gate_up, trainer_down.T,
    )


def solution(mesh):
    in_specs = (
        P("ctx", None, None),
        P("ctx"),
        P("ctx"),
        P(),
        P(("mp", "rep")),
        P(),
        P(),
        P(None, ("ctx", "mp"), None),
        P(None, ("ctx", "mp")),
        P(None, ("ctx", "mp"), None),
        P(None, ("ctx", "mp")),
    )
    out_specs = P(("ctx", "rep"), "mp")
    return jax.shard_map(shards, mesh=mesh, in_specs=in_specs, out_specs=out_specs, check_vma=False)
```

time: 252 us -> 175 us (0.69)
  waiting for transfers between devices: 55.8 us -> 0 us
  Pallas kernels: 126 us -> 170 us
  blocking collectives: 16.2 us -> 0 us
  between operations: 14.7 us -> 0.01 us
  other arithmetic: 13.7 us -> 0 us
  local copies, waits for them, and re-layouts: 14.8 us -> 1.87 us
  starting transfers between devices: 5.1 us -> 0 us
  matrix products: 4.43 us -> 0 us
    all_gather x3 -> x0, waiting for transfers between devices: 53.6 us -> none  [the longest x1 53.4 us: shards(): ffn = lax.all_gather(feed, 'ctx', axis=0)]
    pallas_call x3 -> x1, Pallas kernels: 126 us -> 170 us  [shards(): pl.pallas_call(functools.partial(layer_kernel, n_ctx, pages), out_shape=j...]
    all_to_all x1 -> x0, blocking collectives: 16.2 us -> none  [shards(): feed = lax.all_to_all(feed, 'mp', split_axis=0, concat_axis=0, tiled=True)]
    gather x2 -> x0, local copies, waits for them, and re-layouts: 8.2 us -> none  [the longest x1 5.06 us: shards(): ordered = jnp.take(token_pages, page_table, axis=0).reshape(tokens, D)]
    all_to_all x1 -> x0, starting transfers between devices: 5.01 us -> none  [shards(): got = lax.all_to_all(mixer, 'mp', split_axis=0, concat_axis=0, tiled=True)]
    convert_element_type x4 -> x0, other arithmetic: 4.48 us -> none  [the longest x1 3.41 us: shards(): normed = (wide * lax.rsqrt(jnp.mean(wide * wide, axis=-1, keepdims=True)...]
    dot_general x2 -> x0, matrix products: 4.43 us -> none  [the longest x1 2.33 us: shards(): return jnp.dot(final, order, preferred_element_type=F32).astype(BF16)]
    reduce_sum x2 -> x0, other arithmetic: 4.13 us -> none  [the longest x1 3.5 us: shards(): jnp.mean(wide * wide, axis=-1, keepdims=True) + EPS]
  transfers between devices with their start and end apart: 4 -> 0, of which waited for: 3 -> 0; matrix products, arithmetic and copies ran while one was open for 11% -> 0% of each run, Pallas kernels for 35% -> 0%
where the time goes in v2:
time: 175 us; the launch traced here: 172 us
  Pallas kernels  170 us (97%)
  local copies, waits for them, and re-layouts  1.87 us (1%)
    pallas_call x1, Pallas kernels, shards(): pl.pallas_call(functools.partial(layer_kernel, n_ctx, pages), out_shape=j...  170 us

profile of v2, /device:TPU:1, one launch (start us, length us, event | category | flops | bytes accessed | tf_op | source)
XLA Modules:
  0.0 171.6 jit_solution(8857723726978448510)
XLA Ops:
  0.0 169.8 %layer.1 = bf16[512,512]{1,0:T(8,128)(2,1)} custom-call(s32[8]{0:T(128)} %pt_ref.1, s32[8]{0:T(128)} %live_ref.1, s32[32]{0:T(128)} %len_ref.1, bf16[8,128,2048]{2,1,0:T(8,128)(2,1)} %tok_ref.1, f32[1,256]{1,0:T(1,128)} %bitcast.9, f32[1,2048]{1,0:T(1,128)} %bitcast.7, f32[1,2048]{1,0:T(1,128)} %bitcast.8, f32[3,32,2048]{2,1,0:T(8,128)} %tin_ref.1, ...), custom_call_target="tpu_custom_call" | custom-call | tf_op jit(solution)/shard_map/layer/pallas_call | solution.py:639
  169.8 1.9 %copy.13 = bf16[512,512]{1,0:T(8,128)(2,1)} copy(bf16[512,512]{1,0:T(8,128)(2,1)} %layer.1) | data formatting | bytes 1048576

commit v3 on v2

--- a/solution.py
+++ b/solution.py
@@ -75,31 +75,22 @@
 
 
 class Bulk:
-    def __init__(self, w, pack, both, ysend, yrecv, zsend, zrecv, xsend, xrecv, csend, crecv):
-        self.w, self.pack, self.both = w, pack, both
+    def __init__(self, w, pack, ysend, yrecv, zsend, zrecv, xsend, xrecv, csend, crecv):
+        self.w, self.pack = w, pack
         self.ys, self.yr, self.zs, self.zr = ysend, yrecv, zsend, zrecv
         self.xs, self.xr, self.cs, self.cr = xsend, xrecv, csend, crecv
         self.started = []
-        n_ctx = lax.axis_size("ctx")
-        self.n_z = n_ctx // 4
-        c = lax.axis_index("ctx")
-        self.core, self.z, self.x = lax.rem(c, 2), lax.rem(c // 2, self.n_z), c // (2 * self.n_z)
+        self.at = Place()
         self.mp, self.me = lax.axis_size("mp"), lax.axis_index("mp")
-        self.rep = lax.axis_index("rep")
         self.rows = w.shape[2]
         self.top, self.bottom = pl.ds(0, self.rows // 2), pl.ds(self.rows // 2, self.rows // 2)
         self.all = pl.ds(0, self.rows)
 
-    def ctx(self, xr=0, dz=0, other=0):
-        x = self.x if xr == 0 else 1 - self.x
-        core = self.core if other == 0 else 1 - self.core
-        return x * (2 * self.n_z) + lax.rem(self.z + dz + self.n_z, self.n_z) * 2 + core
-
     def owner(self, i):
         return lax.rem(self.me + self.mp - (0, 1, 3, 2)[i], self.mp) if self.pack is not None else 0
 
     def piece(self, i, rows, xr=0, zr=0, other=0):
-        return self.w.at[self.ctx(xr, (0, -1, 1, 2)[zr], other), self.owner(i), rows, :]
+        return self.w.at[self.at.ctx(xr, (0, -1, 1, 2)[zr], other), self.owner(i), rows, :]
 
     def go(self, copy):
         copy.start()
@@ -109,70 +100,63 @@
         d = (0, 1, 3, 2)[i]
         to = lax.rem(self.me + d, self.mp)
         return remote(
-            self.pack.at[to], self.w.at[self.ctx(), self.me], self.ys.at[i - 1], self.yr.at[i - 1],
-            mp=to,
+            self.pack.at[to], self.w.at[self.at.ctx(), self.me], self.ys.at[i - 1],
+            self.yr.at[i - 1], mp=to,
         )
 
     def y_start(self):
         for i in (1, 2, 3):
             self.go(self.y_copy(i))
 
-    def z_copy(self, i, k, zr, rows):
-        ref = self.piece(i, rows, 0, zr)
-        to = self.ctx(0, 1 if k in (0, 2) else -1)
-        return remote(ref, ref, self.zs.at[i, k], self.zr.at[i, k], ctx=to)
+    def z_copy(self, i, xr, k, zr, rows):
+        ref = self.piece(i, rows, xr, zr)
+        to = self.at.ctx(0, 1 if k in (0, 2) else -1)
+        return remote(ref, ref, self.zs.at[i, xr, k], self.zr.at[i, xr, k], ctx=to)
 
     def x_copies(self, i, zr, xr):
-        if self.both:
-            a, b = self.piece(i, self.top, xr, zr), self.piece(i, self.bottom, xr, zr)
-        else:
-            a, b = self.piece(i, self.all, xr, zr), None
-        out = [remote(a, a, self.xs.at[i, zr, 0], self.xr.at[i, zr, 0], ctx=self.ctx(1))]
-        if b is not None:
-            out.append(
-                remote(
-                    b, b, self.xs.at[i, zr, 1], self.xr.at[i, zr, 1],
-                    ctx=self.ctx(1), rep=1 - self.rep,
-                )
-            )
-        return out
+        a, b = self.piece(i, self.top, xr, zr), self.piece(i, self.bottom, xr, zr)
+        return [
+            remote(a, a, self.xs.at[i, zr, 0], self.xr.at[i, zr, 0], **self.at.same()),
+            remote(b, b, self.xs.at[i, zr, 1], self.xr.at[i, zr, 1], **self.at.cross()),
+        ]
 
     def c_copy(self, i, xr, zr, other=0):
         ref = self.piece(i, self.all, xr, zr, other)
         return remote(
-            ref, ref, self.cs.at[i, xr, zr], self.cr.at[i, xr, zr], ctx=self.ctx(0, 0, 1)
+            ref, ref, self.cs.at[i, xr, zr], self.cr.at[i, xr, zr], **self.at.sibling()
         )
 
-    def onward(self, i, zr):
+    def x_go(self, i, zr):
         for copy in self.x_copies(i, zr, 0):
             self.go(copy)
-        self.go(self.c_copy(i, 0, zr))
-
-    def z_start(self, i):
-        if i:
-            self.y_copy(i).wait_recv()
-        self.go(self.z_copy(i, 0, 0, self.all))
-        self.go(self.z_copy(i, 1, 0, self.all))
-        self.onward(i, 0)
-
-    def z_relay(self, i):
-        self.z_copy(i, 0, 1, self.all).wait_recv()
-        self.go(self.z_copy(i, 2, 1, self.top))
-        self.z_copy(i, 1, 2, self.all).wait_recv()
-        self.go(self.z_copy(i, 3, 2, self.bottom))
-        self.onward(i, 1)
-        self.onward(i, 2)
-
-    def z_far(self, i):
-        self.z_copy(i, 2, 3, self.top).wait_recv()
-        self.z_copy(i, 3, 3, self.bottom).wait_recv()
-        self.onward(i, 3)
 
     def x_take(self, i, zr):
         for copy in self.x_copies(i, zr, 1):
             copy.wait_recv()
         self.go(self.c_copy(i, 1, zr))
 
+    def y_take(self, i):
+        self.y_copy(i).wait_recv()
+
+    def z_start(self, i, xr=0):
+        self.go(self.z_copy(i, xr, 0, 0, self.all))
+        self.go(self.z_copy(i, xr, 1, 0, self.all))
+        if xr == 0:
+            self.go(self.c_copy(i, 0, 0))
+
+    def z_relay(self, i, xr=0):
+        self.z_copy(i, xr, 0, 1, self.all).wait_recv()
+        self.go(self.z_copy(i, xr, 2, 1, self.top))
+        self.go(self.c_copy(i, xr, 1))
+        self.z_copy(i, xr, 1, 2, self.all).wait_recv()
+        self.go(self.z_copy(i, xr, 3, 2, self.bottom))
+        self.go(self.c_copy(i, xr, 2))
+
+    def z_far(self, i, xr=0):
+        self.z_copy(i, xr, 2, 3, self.top).wait_recv()
+        self.z_copy(i, xr, 3, 3, self.bottom).wait_recv()
+        self.go(self.c_copy(i, xr, 3))
+
     def c_take(self, i):
         for xr in range(2):
             for zr in range(4):
@@ -181,6 +165,90 @@
     def drain(self):
         for copy in self.started:
             copy.wait_send()
+
+
+class RepBulk(Bulk):
+    def __init__(self, w, pack, wx, packx, ysx, yrx, zsx, zrx, *sems):
+        super().__init__(w, pack, *sems)
+        self.wx, self.packx = wx, packx
+        self.ysx, self.yrx, self.zsx, self.zrx = ysx, yrx, zsx, zrx
+
+    def extra(self, i, zr):
+        return self.wx.at[self.at.zi((0, -1, 1, 2)[zr]), self.owner(i)]
+
+    def yx_copy(self, i):
+        to = lax.rem(self.me + (0, 1, 3, 2)[i], self.mp)
+        return remote(
+            self.packx.at[to], self.wx.at[self.at.zi(0), self.me], self.ysx.at[i - 1],
+            self.yrx.at[i - 1], mp=to,
+        )
+
+    def y_start(self):
+        for i in (1, 2, 3):
+            self.go(self.y_copy(i))
+            self.go(self.yx_copy(i))
+
+    def y_take(self, i):
+        self.y_copy(i).wait_recv()
+        self.yx_copy(i).wait_recv()
+
+    def zx_copy(self, i, k, zr):
+        ref = self.extra(i, zr)
+        to = self.at.ctx(0, 1 if k == 0 or (k == 2 and i % 2 == 0) else -1)
+        return remote(ref, ref, self.zsx.at[i, k], self.zrx.at[i, k], ctx=to)
+
+    def x_copies(self, i, zr, xr):
+        a = self.piece(i, self.top, xr, zr)
+        b = self.extra(i, zr)
+        dst = self.piece(i, self.bottom, xr, zr)
+        return [
+            remote(a, a, self.xs.at[i, zr, 0], self.xr.at[i, zr, 0], **self.at.same()),
+            remote(b, dst, self.xs.at[i, zr, 1], self.xr.at[i, zr, 1], **self.at.cross()),
+        ]
+
+    def z_start(self, i, xr=0):
+        super().z_start(i)
+        self.go(self.zx_copy(i, 0, 0))
+        self.go(self.zx_copy(i, 1, 0))
+        self.x_go(i, 0)
+
+    def z_relay(self, i, xr=0):
+        super().z_relay(i)
+        self.zx_copy(i, 0, 1).wait_recv()
+        self.zx_copy(i, 1, 2).wait_recv()
+        self.go(self.zx_copy(i, 2, 1 if i % 2 == 0 else 2))
+        self.x_go(i, 1)
+        self.x_go(i, 2)
+
+    def z_far(self, i, xr=0):
+        super().z_far(i)
+        self.zx_copy(i, 2, 3).wait_recv()
+        self.x_go(i, 3)
+
+
+class Place:
+    def __init__(self):
+        c = lax.axis_index("ctx")
+        self.n_z = lax.axis_size("ctx") // 4
+        self.core, self.z, self.x = lax.rem(c, 2), lax.rem(c // 2, self.n_z), c // (2 * self.n_z)
+        self.rep = lax.axis_index("rep")
+
+    def zi(self, dz):
+        return lax.rem(self.z + dz + self.n_z, self.n_z)
+
+    def ctx(self, xr=0, dz=0, other=0):
+        x = self.x if xr == 0 else 1 - self.x
+        core = self.core if other == 0 else 1 - self.core
+        return x * (2 * self.n_z) + self.zi(dz) * 2 + core
+
+    def same(self):
+        return dict(ctx=self.ctx(1))
+
+    def cross(self):
+        return dict(ctx=self.ctx(1), rep=1 - self.rep)
+
+    def sibling(self):
+        return dict(ctx=self.ctx(0, 0, 1))
 
 
 def greet(peers):
@@ -194,18 +262,19 @@
 
 def layer_kernel(
     n_ctx, pages,
-    pt_ref, live_ref, len_ref, tok_ref, floor_ref, mgain_ref, fgain_ref,
-    tin_ref, tout_ref, tgu_ref, tdn_ref,
+    pt_ref, live_ref, len_ref, floor_ref, mgain_ref, fgain_ref,
+    tin_ref, tok_hbm, tout_hbm, tgu_hbm, tdn_hbm,
     out_ref,
-    wq_ref, wo_ref, wf_ref, pkq_ref, pkf_ref, x_ref, ord_ref,
+    tok_ref, tout_ref, tgu_ref, tdn_ref,
+    wq_ref, wqx_ref, wo_ref, wf_ref, pkq_ref, pkqx_ref, pkf_ref, x_ref, ord_ref,
     q_ref, k_ref, v_ref, ctot_ref, cnt_ref, st_ref, dec_ref, run_ref, mix_ref,
-    msg_ref, in_ref, num_ref, nin_ref, oth_ref, head_ref, xall_ref, ss_ref, res_ref,
+    msg_ref, in_ref, num_ref, nin_ref, oth_ref, via_ref, head_ref, xall_ref, ss_ref, res_ref,
     hid_ref, rs_ref, part_ref, send_ref, rin_ref,
     *sems,
 ):
-    (n_ssem, n_rsem, s_sem, r_sem, p_ssem, p_rsem, g_ssem, g_rsem, a_ssem, a_rsem,
-     b_ssem, b_rsem, t_ssem, t_rsem) = sems[:14]
-    sq, so, sf = sems[14:22], sems[22:28], sems[28:36]
+    (l_sem, n_ssem, n_rsem, s_sem, r_sem, p_ssem, p_rsem, g_ssem, g_rsem, a_ssem, a_rsem,
+     b_ssem, b_rsem, t_ssem, t_rsem) = sems[:15]
+    sq, so, sf = sems[15:27], sems[27:33], sems[33:41]
     width = 2 * PAGE
     cols, hid = width, tdn_ref.shape[1] // 4
     ctx, rep = lax.axis_index("ctx"), lax.axis_index("rep")
@@ -213,21 +282,34 @@
     half_pages = pages // 2
     rows = half_pages * PAGE
     wl = tin_ref.shape[1]
-    bq = Bulk(wq_ref, pkq_ref, False, *sq)
-    bo = Bulk(wo_ref, None, True, None, None, *so)
-    bf = Bulk(wf_ref, pkf_ref, True, *sf)
+    at = Place()
+    bq = RepBulk(wq_ref, pkq_ref, wqx_ref, pkqx_ref, *sq)
+    bo = Bulk(wo_ref, None, None, None, *so)
+    bf = Bulk(wf_ref, pkf_ref, *sf)
+    loads = [
+        pltpu.make_async_copy(a, b, l_sem.at[k])
+        for k, (a, b) in enumerate(
+            [(tgu_hbm, tgu_ref), (tdn_hbm, tdn_ref), (tout_hbm, tout_ref), (tok_hbm, tok_ref)]
+        )
+    ]
+    for load in loads:
+        load.start()
 
     for y in range(4):
         for t in range(3):
             lane = pl.multiple_of((y * 2 + rep) * cols, cols)
             pkq_ref[y, :, pl.ds(t * cols, cols)] = tin_ref[t, :, pl.ds(lane, cols)].astype(BF16)
+            lane = pl.multiple_of((y * 2 + 1 - rep) * cols, cols)
+            pkqx_ref[y, :, pl.ds(t * cols, cols)] = tin_ref[
+                t, pl.ds(wl // 2, wl // 2), pl.ds(lane, cols)
+            ].astype(BF16)
     wq_ref[ctx, me] = pkq_ref[me]
-
-    peers = [dict(ctx=lax.rem(ctx + o, n_ctx)) for o in range(1, n_ctx)]
+    wqx_ref[at.z, me] = pkqx_ref[me]
+
     greet(
-        peers
-        + [dict(mp=left), dict(mp=right), dict(mp=far), dict(rep=1 - rep)]
-        + [dict(ctx=bq.ctx(1), rep=1 - rep)]
+        [at.sibling(), at.same(), at.cross()]
+        + [dict(ctx=at.ctx(0, dz)) for dz in (1, 2, 3)]
+        + [dict(mp=left), dict(mp=right), dict(mp=far)]
     )
     bq.y_start()
     bq.z_start(0)
@@ -242,17 +324,16 @@
         upto = jnp.where(row8 == b, so_far * PAGE + flag * (lane8 + 1), upto)
         alive = jnp.where(row8 == b, flag.astype(F32), alive)
         so_far = so_far + flag
-    num_ref[...] = jnp.zeros((pages, PAGE), jnp.int32) + so_far * PAGE
-
-    def num_copy(o):
-        return remote(
-            num_ref, nin_ref.at[o - 1], n_ssem.at[o - 1], n_rsem.at[o - 1],
-            ctx=lax.rem(ctx + o, n_ctx),
-        )
-
-    for o in range(1, n_ctx):
-        num_copy(o).start()
-
+    def num_copy(k):
+        to = at.sibling() if k == 0 else at.same() if k == 4 else dict(ctx=at.ctx(0, k))
+        src = num_ref.at[0 if k == 0 else 2 if k == 4 else 1]
+        return remote(src, nin_ref.at[k], n_ssem.at[k], n_rsem.at[k], **to)
+
+    num_ref[0] = jnp.zeros((pages, PAGE), jnp.int32) + so_far * PAGE
+    num_copy(0).start()
+
+    for load in loads[:3]:
+        load.wait()
     wo_ref[ctx, 0] = tout_ref[...].astype(BF16)
     for y in range(4):
         for j in range(hid // PAGE):
@@ -263,6 +344,9 @@
         pkf_ref[y, :, pl.ds(2 * hid, hid)] = tdn_ref[:, pl.ds(y * hid, hid)].astype(BF16)
     wf_ref[ctx, me] = pkf_ref[me]
     bf.y_start()
+    bf.x_go(0, 0)
+    bo.x_go(0, 0)
+    loads[3].wait()
 
     def norm(b):
         x = tok_ref[pt_ref[b]].astype(F32)
@@ -287,32 +371,45 @@
             ord_ref[pl.ds(j * PAGE, PAGE), pl.ds(t * PAGE, PAGE)] = tile
 
     norm(0)
+    bq.y_take(1)
     bq.z_start(1)
+    bq.y_take(2)
     bq.z_start(2)
-    bo.z_start(0)
-    bf.z_start(0)
+    num_copy(0).wait_recv()
+    num_ref[1] = num_ref[0] + nin_ref[0]
+    for k in (1, 2, 3):
+        num_copy(k).start()
     norm(1)
     norm(2)
+    bq.y_take(3)
     bq.z_start(3)
     bq.z_relay(0)
     norm(3)
+    for k in (1, 2, 3):
+        num_copy(k).wait_recv()
+    num_ref[2] = num_ref[1] + nin_ref[1] + nin_ref[2] + nin_ref[3]
+    num_copy(4).start()
+    norm(4)
     bq.z_relay(1)
     bq.z_relay(2)
-    norm(4)
     norm(5)
+    norm(6)
     bq.z_relay(3)
+    bf.z_start(0)
+    bo.z_start(0)
+    norm(7)
     bq.z_far(0)
-    norm(6)
     bq.z_far(1)
     bq.z_far(2)
-    norm(7)
     bq.z_far(3)
-
-    for o in range(1, n_ctx):
-        num_copy(o).wait_recv()
-    base = jnp.zeros((pages, PAGE), jnp.int32)
-    for o in range(1, n_ctx):
-        base = base + jnp.where(o <= ctx, nin_ref[o - 1], 0)
+    bf.x_take(0, 0)
+    bf.z_start(0, 1)
+    bo.x_take(0, 0)
+    bo.z_start(0, 1)
+    num_copy(4).wait_recv()
+    base = jnp.where(at.core == 1, nin_ref[0], 0) + jnp.where(at.x == 1, nin_ref[4], 0)
+    for k in (1, 2, 3):
+        base = base + jnp.where(k <= at.z, nin_ref[k], 0)
     count = jnp.zeros((pages, PAGE), F32)
     start = jnp.int32(0)
     for j in range(len_ref.shape[0]):
@@ -378,37 +475,43 @@
                 add = dot(v_ref[here, lanes], ke[:, lanes], TN)
                 run_ref[h] = state * decay[:, lanes] + add
 
+    def block_in(ref):
+        tail = ref[pl.ds(PAGE, 16), :].astype(F32)
+        return ref[pl.ds(0, PAGE), :].astype(F32), tail[0:1, :] + tail[1:2, :]
+
+    def block_out(ref, block):
+        state, decay = block
+        ref[pl.ds(0, PAGE), :] = state.astype(BF16)
+        hi = decay.astype(BF16)
+        lo = (decay - hi.astype(F32)).astype(BF16)
+        line = lax.broadcasted_iota(jnp.int32, (16, PAGE), 0)
+        both = jnp.where(line == 0, hi.astype(F32), jnp.where(line == 1, lo.astype(F32), 0.0))
+        ref[pl.ds(PAGE, 16), :] = both.astype(BF16)
+
+    def join(early, late):
+        return early[0] * late[1] + late[0], early[1] * late[1]
+
+    def choose(flag, a, b):
+        return jnp.where(flag, a[0], b[0]), jnp.where(flag, a[1], b[1])
+
+    def state_copy(k):
+        to = at.sibling() if k in (0, 5) else at.same() if k == 4 else dict(ctx=at.ctx(0, k))
+        src = msg_ref.at[{0: 0, 4: 2, 5: 3}.get(k, 1)]
+        return remote(src, in_ref.at[k], s_sem.at[k], r_sem.at[k], **to)
+
+    def local_block(h):
+        return run_ref[h], dec_ref[:, pl.ds(pl.multiple_of(h * PAGE, PAGE), PAGE)]
+
     project(0)
+    bf.y_take(1)
     bf.z_start(1)
-    bf.z_start(2)
+    bf.x_go(1, 0)
     project(1)
-    bf.z_start(3)
+    project(2)
     bo.z_relay(0)
-    bf.z_relay(0)
-    project(2)
-    bo.z_far(0)
-    bf.z_relay(1)
     project(3)
-
-    dec = dec_ref[...]
-    for h in range(2):
-        lanes = slice(h * PAGE, (h + 1) * PAGE)
-        msg_ref[h, pl.ds(0, PAGE), :] = run_ref[h].astype(BF16)
-        hi = dec[:, lanes].astype(BF16)
-        lo = (dec[:, lanes] - hi.astype(F32)).astype(BF16)
-        first = lax.broadcasted_iota(jnp.int32, (16, PAGE), 0)
-        both = jnp.where(first == 0, hi.astype(F32), jnp.where(first == 1, lo.astype(F32), 0.0))
-        msg_ref[h, pl.ds(PAGE, 16), :] = both.astype(BF16)
-
-    def state_copy(o):
-        return remote(
-            msg_ref, in_ref.at[o - 1], s_sem.at[o - 1], r_sem.at[o - 1],
-            ctx=lax.rem(ctx + o, n_ctx),
-        )
-
-    for o in range(1, n_ctx):
-        state_copy(o).start()
-    bf.z_relay(2)
+    block_out(msg_ref.at[0], local_block(1 - at.core))
+    state_copy(0).start()
 
     def within(b, _):
         here = pl.ds(pl.multiple_of(b * PAGE, PAGE), PAGE)
@@ -421,28 +524,40 @@
             mix_ref[here, lanes] = dot(scores, v_ref[here, lanes])
         return 0
 
-    lax.fori_loop(0, pages, within, 0)
-    bf.z_relay(3)
-    bf.z_far(0)
+    lax.fori_loop(0, 2, within, 0)
+    state_copy(0).wait_recv()
+    own, sib = local_block(at.core), block_in(in_ref.at[0])
+    first, second = choose(at.core == 0, own, sib), choose(at.core == 0, sib, own)
+    chip = join(first, second)
+    block_out(msg_ref.at[1], chip)
+    for k in (1, 2, 3):
+        state_copy(k).start()
+    lax.fori_loop(2, pages, within, 0)
+    for k in (1, 2, 3):
+        state_copy(k).wait_recv()
+    whole = (jnp.zeros((PAGE, PAGE), F32), jnp.ones((1, PAGE), F32))
+    ahead = whole
+    for z in range(at.n_z):
+        there = block_in(msg_ref.at[1])
+        for k in (1, 2, 3):
+            there = choose(lax.rem(at.z + at.n_z - z, at.n_z) == k, block_in(in_ref.at[k]), there)
+        whole = join(whole, there)
+        ahead = choose(z < at.z, whole, ahead)
+    block_out(msg_ref.at[2], whole)
+    state_copy(4).start()
+    bf.z_relay(0, 0)
+    bf.z_relay(0, 1)
     for j in range(half_pages):
         pick(j)
-
-    for o in range(1, n_ctx):
-        state_copy(o).wait_recv()
-    run_ref[...] = jnp.zeros_like(run_ref)
-
-    def fold(i, _):
-        o = n_ctx - 1 - i
-        ahead = jnp.where(o <= ctx, 1.0, 0.0)
-        for h in range(2):
-            tail = in_ref[o - 1, h, pl.ds(PAGE, 16), :].astype(F32)
-            decay = tail[0:1, :] + tail[1:2, :]
-            state = run_ref[h]
-            longer = state * decay + in_ref[o - 1, h, pl.ds(0, PAGE), :].astype(F32)
-            run_ref[h] = state + ahead * (longer - state)
-        return 0
-
-    lax.fori_loop(0, n_ctx - 1, fold, 0)
+    state_copy(4).wait_recv()
+    before = choose(at.x == 1, block_in(in_ref.at[4]), (jnp.zeros((PAGE, PAGE), F32), jnp.ones((1, PAGE), F32)))
+    enter0 = join(before, ahead)
+    enter1 = join(enter0, first)
+    block_out(msg_ref.at[3], choose(at.core == 0, enter1, enter0))
+    state_copy(5).start()
+    run_ref[at.core] = choose(at.core == 0, enter0, enter1)[0]
+    state_copy(5).wait_recv()
+    run_ref[1 - at.core] = block_in(in_ref.at[5])[0]
 
     def outputs(b, dst, dst_row, dst_lane):
         here = pl.ds(pl.multiple_of(b * PAGE, PAGE), PAGE)
@@ -466,10 +581,25 @@
     def lane_of(owner, which):
         return pl.multiple_of((owner * 2 + which) * width, width)
 
-    swap = remote(
-        oth_ref, head_ref.at[:, pl.ds(lane_of(me, rep), width)], p_ssem, p_rsem, rep=1 - rep
-    )
-    swap.start()
+    quarter = rows // 2
+
+    def swap_out(k):
+        to = at.same() if k == 0 else at.cross()
+        return remote(
+            oth_ref.at[pl.ds(k * quarter, quarter), :], via_ref.at[k], p_ssem.at[k], p_rsem.at[k], **to
+        )
+
+    def swap_on(k):
+        to = at.cross() if k == 0 else at.same()
+        which = rep if k == 0 else 1 - rep
+        return remote(
+            via_ref.at[k],
+            head_ref.at[pl.ds(k * quarter, quarter), pl.ds(lane_of(me, which), width)],
+            p_ssem.at[2 + k], p_rsem.at[2 + k], **to,
+        )
+
+    swap_out(0).start()
+    swap_out(1).start()
     mine = lane_of(me, rep)
 
     def own_half(j, _):
@@ -484,18 +614,40 @@
     ring_a = Ring(view(rep), rows, g_ssem, g_rsem, 0)
     ring_b = Ring(view(1 - rep), rows, g_ssem, g_rsem, 4)
     ring_a.start()
+    swap_out(0).wait_recv()
+    swap_on(0).start()
+    swap_out(1).wait_recv()
+    swap_on(1).start()
+    bf.y_take(2)
+    bf.z_start(2)
+    bf.z_far(0, 0)
+    bf.z_far(0, 1)
+    bo.z_relay(0, 1)
+    bo.z_far(0)
+    bf.x_go(2, 0)
+    bf.z_relay(1)
+    bf.x_go(1, 1)
+    swap_on(0).wait_recv()
+    swap_on(1).wait_recv()
+    ring_b.start()
+    ring_a.relay()
+    bf.y_take(3)
+    bf.z_start(3)
+    bf.x_go(1, 2)
+    bf.x_go(3, 0)
+    bf.z_relay(2)
+    bf.x_go(2, 1)
+    ring_b.relay()
+    bo.z_far(0, 1)
     bf.z_far(1)
-    swap.wait_recv()
-    ring_b.start()
+    bf.x_go(1, 3)
+    bf.z_relay(3)
+    bf.x_go(2, 2)
+    bf.x_go(3, 1)
+    bf.x_go(3, 2)
     bf.z_far(2)
-    ring_a.relay()
-    bf.z_far(3)
-    for zr in range(4):
-        bo.x_take(0, zr)
-    ring_b.relay()
+    bf.x_go(2, 3)
     bo.c_take(0)
-    for zr in range(4):
-        bf.x_take(0, zr)
     gain = jnp.concatenate(
         [my_columns(lambda c: jnp.broadcast_to(fgain_ref[:, pl.ds(c * PAGE, PAGE)], (8, PAGE)), t)[0:1] for t in range(4)],
         axis=1,
@@ -519,9 +671,7 @@
     ss_copy(0, me, right).start()
     ss_copy(1, me, left).start()
     ord_ref[...] = res
-    for i in range(1, 4):
-        for zr in range(4):
-            bf.x_take(i, zr)
+    ord_ref[...] = res
     for t in range(4):
         tile = ord_ref[:, pl.ds(t * PAGE, PAGE)]
         for k in range(4):
@@ -531,6 +681,11 @@
     ss_copy(0, left, right).wait_recv()
     ss_copy(2, left, right).start()
     ss_copy(1, right, left).wait_recv()
+    bf.z_far(3)
+    bf.x_go(3, 3)
+    for i in range(1, 4):
+        for zr in range(4):
+            bf.x_take(i, zr)
     for i in range(4):
         bf.c_take(i)
     ss_copy(2, far, right).wait_recv()
@@ -605,15 +760,19 @@
     ss_copy(0, me, right).wait_send()
     ss_copy(1, me, left).wait_send()
     ss_copy(2, left, right).wait_send()
-    swap.wait_send()
-    for o in range(1, n_ctx):
-        state_copy(o).wait_send()
-        num_copy(o).wait_send()
+    for k in range(2):
+        swap_out(k).wait_send()
+        swap_on(k).wait_send()
+    for k in range(6):
+        state_copy(k).wait_send()
+    for k in range(5):
+        num_copy(k).wait_send()
     for bulk in (bq, bo, bf):
         bulk.drain()
 
 
 VM = pl.BlockSpec(memory_space=pltpu.VMEM)
+HB = pl.BlockSpec(memory_space=pl.ANY)
 SM = pl.BlockSpec(memory_space=pltpu.SMEM)
 
 
@@ -633,19 +792,26 @@
     def bulk_sems(n, y):
         near = [dma((3,)), dma((3,))] if y else []
         return near + [
-            dma((n, 4)), dma((n, 4)), dma((n, 4, 2)), dma((n, 4, 2)), dma((n, 2, 4)), dma((n, 2, 4)),
+            dma((n, 2, 4)), dma((n, 2, 4)), dma((n, 4, 2)), dma((n, 4, 2)),
+            dma((n, 2, 4)), dma((n, 2, 4)),
         ]
 
     return pl.pallas_call(
         functools.partial(layer_kernel, n_ctx, pages),
         out_shape=jax.ShapeDtypeStruct((half, block), BF16),
-        in_specs=[SM, SM, SM] + [VM] * 8,
+        in_specs=[SM, SM, SM] + [VM] * 4 + [HB] * 4,
         out_specs=VM,
         scratch_shapes=[
+            pltpu.VMEM((pages, page, D), BF16),
+            pltpu.VMEM((wl, D), F32),
+            pltpu.VMEM((2, wl, 4 * hid), F32),
+            pltpu.VMEM((wl, 4 * hid), F32),
             pltpu.VMEM((n_ctx, 4, wl, 3 * cols), BF16),
+            pltpu.VMEM((4, 4, wl // 2, 3 * cols), BF16),
             pltpu.VMEM((n_ctx, 1, wl, D), BF16),
             pltpu.VMEM((n_ctx, 4, wl, 3 * hid), BF16),
             pltpu.VMEM((4, wl, 3 * cols), BF16),
+            pltpu.VMEM((4, wl // 2, 3 * cols), BF16),
             pltpu.VMEM((4, wl, 3 * hid), BF16),
             pltpu.VMEM((tokens, D), BF16),
             pltpu.VMEM((half, block), F32),
@@ -658,11 +824,12 @@
             pltpu.VMEM((1, cols), F32),
             pltpu.VMEM((2, PAGE, PAGE), F32),
             pltpu.VMEM((tokens, cols), F32),
-            pltpu.VMEM((2, PAGE + 16, PAGE), BF16),
-            pltpu.VMEM((n_ctx - 1, 2, PAGE + 16, PAGE), BF16),
-            pltpu.VMEM((pages, PAGE), jnp.int32),
-            pltpu.VMEM((n_ctx - 1, pages, PAGE), jnp.int32),
+            pltpu.VMEM((4, PAGE + 16, PAGE), BF16),
+            pltpu.VMEM((6, PAGE + 16, PAGE), BF16),
+            pltpu.VMEM((3, pages, PAGE), jnp.int32),
+            pltpu.VMEM((5, pages, PAGE), jnp.int32),
             pltpu.VMEM((half, cols), BF16),
+            pltpu.VMEM((2, half // 2, cols), BF16),
             pltpu.VMEM((half, D), BF16),
             pltpu.VMEM((4, half, block), BF16),
             pltpu.VMEM((4, 8, half), F32),
@@ -672,19 +839,20 @@
             pltpu.VMEM((half, block), F32),
             pltpu.VMEM((3, half, block), BF16),
             pltpu.VMEM((4, half, block), BF16),
-            dma((n_ctx - 1,)), dma((n_ctx - 1,)), dma((n_ctx - 1,)), dma((n_ctx - 1,)),
-            dma(()), dma(()), dma((8,)), dma((8,)), dma((4,)), dma((4,)),
+            dma((4,)), dma((5,)), dma((5,)), dma((6,)), dma((6,)),
+            dma((4,)), dma((4,)), dma((8,)), dma((8,)), dma((4,)), dma((4,)),
             dma((3,)), dma((3,)), dma((4,)), dma((4,)),
         ]
+        + [dma((3,)), dma((3,)), dma((4, 3)), dma((4, 3))]
         + bulk_sems(4, True) + bulk_sems(1, False) + bulk_sems(4, True),
         compiler_params=pltpu.CompilerParams(
             collective_id=0, has_side_effects=True, vmem_limit_bytes=VMEM_LIMIT
         ),
         name="layer",
     )(
-        page_table, live_flags, lengths, token_pages, decay_floor.reshape(1, cols),
+        page_table, live_flags, lengths, decay_floor.reshape(1, cols),
         mixer_gain.reshape(1, D), feed_gain.reshape(1, D),
-        trainer_mixer_in, trainer_mixer_out.T, trainer_gate_up, trainer_down.T,
+        trainer_mixer_in, token_pages, trainer_mixer_out.T, trainer_gate_up, trainer_down.T,
     )
 
 

time: 175 us -> 142 us (0.81); the launches traced: 172 us -> 142 us
  Pallas kernels: 170 us -> 140 us
    pallas_call x1, Pallas kernels: 170 us -> 140 us  [shards(): pl.pallas_call(functools.partial(layer_kernel, n_ctx, pages), out_shape=j...]
where the time goes in v3:
time: 142 us
  Pallas kernels  140 us (99%)
  local copies, waits for them, and re-layouts  1.87 us (1%)
    pallas_call x1, Pallas kernels, shards(): pl.pallas_call(functools.partial(layer_kernel, n_ctx, pages), out_shape=j...  140 us

profile of v3, /device:TPU:1, one launch (start us, length us, event | category | flops | bytes accessed | tf_op | source)
XLA Modules:
  0.0 141.6 jit_solution(4270843380120716829)
XLA Ops:
  0.0 139.7 %layer.1 = bf16[512,512]{1,0:T(8,128)(2,1)} custom-call(s32[8]{0:T(128)} %pt_ref.1, s32[8]{0:T(128)} %live_ref.1, s32[32]{0:T(128)} %len_ref.1, f32[1,256]{1,0:T(1,128)} %bitcast.9, f32[1,2048]{1,0:T(1,128)} %bitcast.7, f32[1,2048]{1,0:T(1,128)} %bitcast.8, f32[3,32,2048]{2,1,0:T(8,128)} %tin_ref.1, bf16[8,128,2048]{2,1,0:T(8,128)(2,1)} %tok_hbm.1, ...), custom_call_target="tpu_custom_call" | custom-call | tf_op jit(solution)/shard_map/layer/pallas_call | solution.py:799
  139.7 1.9 %copy.13 = bf16[512,512]{1,0:T(8,128)(2,1)} copy(bf16[512,512]{1,0:T(8,128)(2,1)} %layer.1) | data formatting | bytes 1048576

commit v4 on v3

v4 whole, which is shorter than its diff:
```python
import functools

import jax
import jax.numpy as jnp
from jax import lax
from jax.experimental import pallas as pl
from jax.experimental.pallas import tpu as pltpu
from jax.sharding import PartitionSpec as P

D = 2048
HEADS = 16
PAGE = 128
EPS = 1e-05
VMEM_LIMIT = 67043328
NT = (((1,), (1,)), ((), ()))
TN = (((0,), (0,)), ((), ()))
F32 = jnp.float32
BF16 = jnp.bfloat16


def remote(src, dst, ssem, rsem, **where):
    return pltpu.make_async_remote_copy(
        src_ref=src,
        dst_ref=dst,
        send_sem=ssem,
        recv_sem=rsem,
        device_id=where,
        device_id_type=pl.DeviceIdType.MESH,
    )


def dot(a, b, dims=None):
    if dims is None:
        return jnp.dot(a, b, preferred_element_type=F32)
    return lax.dot_general(a, b, dims, preferred_element_type=F32)


def ring_neighbours():
    mp = lax.axis_size("mp")
    me = lax.axis_index("mp")
    return lax.rem(me + mp - 1, mp), me, lax.rem(me + 1, mp), lax.rem(me + 2, mp)


class Ring:
    def __init__(self, view, rows, whole, ssem, rsem, n):
        self.view, self.half, self.whole = view, rows // 2, whole
        self.ssem, self.rsem, self.n = ssem, rsem, n

    def copy(self, owner, part, k):
        left, _, right, _ = ring_neighbours()
        ref = self.view(owner, part * self.half, self.half)
        return remote(
            ref, ref, self.ssem.at[self.n], self.rsem.at[self.n, k // 2],
            mp=right if k % 2 == 0 else left,
        )

    def take(self, stage):
        left, _, right, _ = ring_neighbours()
        ref = self.view(0, 0, 2 * self.half)
        remote(ref, ref, self.ssem.at[self.n], self.rsem.at[self.n, stage], mp=right).wait_recv()

    def start(self):
        _, me, _, _ = ring_neighbours()
        for k, part in enumerate((0, 1, 1, 0)):
            self.copy(me, part, k).start()

    def relay(self):
        left, _, right, _ = ring_neighbours()
        self.take(0)
        self.copy(left, 0, 4).start()
        self.copy(right, 1, 5).start()

    def near(self):
        self.take(1)

    def finish(self):
        _, _, right, _ = ring_neighbours()
        self.take(2)
        remote(
            self.whole, self.whole, self.ssem.at[self.n], self.rsem.at[self.n, 2], mp=right
        ).wait_send()


class Bulk:
    def __init__(self, hold, w, pack, ysend, yrecv, send, near, far, xrecv, crecv):
        self.w, self.pack = w, pack
        self.ys, self.yr, self.send, self.zn, self.zf = ysend, yrecv, send, near, far
        self.xr, self.cr = xrecv, crecv
        self.pending, self.hold = [], hold
        self.at = Place()
        self.mp, self.me = lax.axis_size("mp"), lax.axis_index("mp")
        self.rows = w.shape[2]
        self.top, self.bottom = pl.ds(0, self.rows // 2), pl.ds(self.rows // 2, self.rows // 2)
        self.all = pl.ds(0, self.rows)

    def span(self, n):
        if self.w.shape[1] == 1:
            return self.w.at[pl.ds(0, n)]
        return self.w.at[0, pl.ds(0, n)] if n < 4 else self.w.at[pl.ds(0, n // 4)]

    def wait_in(self, ref, sem):
        remote(ref, ref, self.send, sem, **self.at.sibling()).wait_recv()

    def wait_out(self, ref, sem):
        remote(ref, ref, sem, self.cr.at[0], **self.at.sibling()).wait_send()

    def owner(self, i):
        return lax.rem(self.me + self.mp - (0, 1, 3, 2)[i], self.mp) if self.pack is not None else 0

    def piece(self, i, rows, xr=0, zr=0, other=0):
        return self.w.at[self.at.ctx(xr, (0, -1, 1, 2)[zr], other), self.owner(i), rows, :]

    def go(self, copy):
        copy.start()

    def y_copy(self, i):
        d = (0, 1, 3, 2)[i]
        to = lax.rem(self.me + d, self.mp)
        return remote(
            self.pack.at[to], self.w.at[self.at.ctx(), self.me], self.ys, self.yr.at[i - 1], mp=to,
        )

    def y_start(self, which=(1, 2, 3)):
        for i in which:
            self.go(self.y_copy(i))

    def z_copy(self, i, xr, k, zr, rows):
        ref = self.piece(i, rows, xr, zr)
        to = self.at.ctx(0, 1 if k in (0, 2) else -1)
        got = (self.zn if k < 2 else self.zf).at[i, xr]
        return remote(ref, ref, self.send, got, ctx=to)

    def x_copies(self, i, zr, xr):
        a, b = self.piece(i, self.top, xr, zr), self.piece(i, self.bottom, xr, zr)
        return [
            remote(a, a, self.send, self.xr.at[i, zr], **self.at.same()),
            remote(b, b, self.send, self.xr.at[i, zr], **self.at.cross()),
        ]

    def c_sem(self, i, xr):
        return self.cr.at[i]

    def c_copy(self, i, xr, zr):
        ref = self.piece(i, self.all, xr, zr)
        return remote(ref, ref, self.send, self.c_sem(i, xr), **self.at.sibling())

    def c_go(self, i, xr, zr):
        if self.hold:
            self.pending.append((i, xr, zr))
        else:
            self.go(self.c_copy(i, xr, zr))

    def flush(self, hold):
        for piece in self.pending:
            self.go(self.c_copy(*piece))
        self.pending, self.hold = [], hold

    def x_go(self, i, zr):
        for copy in self.x_copies(i, zr, 0):
            self.go(copy)

    def x_take(self, i, zr):
        self.wait_in(self.piece(i, self.all, 1, zr), self.xr.at[i, zr])
        self.c_go(i, 1, zr)

    def y_take(self, i):
        self.y_copy(i).wait_recv()

    def z_start(self, i, xr=0):
        self.go(self.z_copy(i, xr, 0, 0, self.all))
        self.go(self.z_copy(i, xr, 1, 0, self.all))
        if xr == 0:
            self.c_go(i, 0, 0)

    def z_relay(self, i, xr=0):
        self.wait_in(self.span(2), self.zn.at[i, xr])
        self.go(self.z_copy(i, xr, 2, 1, self.top))
        self.go(self.z_copy(i, xr, 3, 2, self.bottom))
        self.c_go(i, xr, 1)
        self.c_go(i, xr, 2)

    def z_far(self, i, xr=0):
        self.wait_in(self.piece(i, self.all, xr, 3), self.zf.at[i, xr])
        self.c_go(i, xr, 3)

    def c_take(self, i):
        self.wait_in(self.span(8), self.cr.at[i])

    def drain(self):
        if self.pack is None:
            self.wait_out(self.span(15), self.send)
        else:
            self.wait_out(self.span(60), self.send)
            self.wait_out(self.span(3), self.ys)


class RepBulk(Bulk):
    def __init__(self, w, pack, wx, packx, ysx, yrx, zsx, znx, zfx, *sems):
        super().__init__(False, w, pack, *sems)
        self.wx, self.packx = wx, packx
        self.ysx, self.yrx, self.zsx, self.znx, self.zfx = ysx, yrx, zsx, znx, zfx

    def extra(self, i, zr):
        return self.wx.at[self.at.zi((0, -1, 1, 2)[zr]), self.owner(i)]

    def yx_copy(self, i):
        to = lax.rem(self.me + (0, 1, 3, 2)[i], self.mp)
        return remote(
            self.packx.at[to], self.wx.at[self.at.zi(0), self.me], self.ysx, self.yrx.at[i - 1],
            mp=to,
        )

    def y_start(self, which=(1, 2, 3)):
        for i in which:
            self.go(self.y_copy(i))
            self.go(self.yx_copy(i))

    def y_take(self, i):
        self.y_copy(i).wait_recv()
        self.yx_copy(i).wait_recv()

    def zx_copy(self, i, k, zr):
        ref = self.extra(i, zr)
        to = self.at.ctx(0, 1 if k == 0 or (k == 2 and i % 2 == 0) else -1)
        return remote(ref, ref, self.zsx, (self.znx if k < 2 else self.zfx).at[i], ctx=to)

    def x_copies(self, i, zr, xr):
        a = self.piece(i, self.top, xr, zr)
        b = self.extra(i, zr)
        dst = self.piece(i, self.bottom, xr, zr)
        return [
            remote(a, a, self.send, self.xr.at[i, zr], **self.at.same()),
            remote(b, dst, self.send, self.xr.at[i, zr], **self.at.cross()),
        ]

    def c_sem(self, i, xr):
        return self.cr.at[xr]

    def c_take(self, xr):
        self.wait_in(self.span(16), self.cr.at[xr])

    def z_start(self, i, xr=0):
        super().z_start(i)
        self.go(self.zx_copy(i, 0, 0))
        self.go(self.zx_copy(i, 1, 0))
        self.x_go(i, 0)

    def z_relay(self, i, xr=0):
        super().z_relay(i)
        self.wait_in(self.wx.at[0, pl.ds(0, 2)], self.znx.at[i])
        self.go(self.zx_copy(i, 2, 1 if i % 2 == 0 else 2))
        self.x_go(i, 1)
        self.x_go(i, 2)

    def z_far(self, i, xr=0):
        super().z_far(i)
        self.zx_copy(i, 2, 3).wait_recv()
        self.x_go(i, 3)

    def drain(self):
        super().drain()
        self.wait_out(self.wx.at[pl.ds(0, 3)], self.zsx)
        self.wait_out(self.wx.at[0, pl.ds(0, 3)], self.ysx)


class Place:
    def __init__(self):
        c = lax.axis_index("ctx")
        self.n_z = lax.axis_size("ctx") // 4
        self.core, self.z, self.x = lax.rem(c, 2), lax.rem(c // 2, self.n_z), c // (2 * self.n_z)
        self.rep = lax.axis_index("rep")

    def zi(self, dz):
        return lax.rem(self.z + dz + self.n_z, self.n_z)

    def ctx(self, xr=0, dz=0, other=0):
        x = self.x if xr == 0 else 1 - self.x
        core = self.core if other == 0 else 1 - self.core
        return x * (2 * self.n_z) + self.zi(dz) * 2 + core

    def same(self):
        return dict(ctx=self.ctx(1))

    def cross(self):
        return dict(ctx=self.ctx(1), rep=1 - self.rep)

    def sibling(self):
        return dict(ctx=self.ctx(0, 0, 1))


def greet(peers):
    barrier = pltpu.get_barrier_semaphore()
    for where in peers:
        pl.semaphore_signal(
            barrier, inc=1, device_id=where, device_id_type=pl.DeviceIdType.MESH
        )
    pl.semaphore_wait(barrier, len(peers))


def layer_kernel(
    n_ctx, pages,
    pt_ref, live_ref, len_ref, floor_ref, mgain_ref, fgain_ref,
    tin_ref, tok_hbm, tout_hbm, tgu_hbm, tdn_hbm,
    out_ref,
    tok_ref, tout_ref, tgu_ref, tdn_ref,
    wq_ref, wqx_ref, wo_ref, wf_ref, pkq_ref, pkqx_ref, pkf_ref, x_ref, ord_ref,
    q_ref, k_ref, v_ref, ctot_ref, cnt_ref, st_ref, dec_ref, run_ref, mix_ref,
    msg_ref, in_ref, num_ref, nin_ref, oth_ref, via_ref, head_ref, xall_ref, ss_ref, res_ref,
    hid_ref, rs_ref, acc_ref, send_ref, rin_ref,
    *sems,
):
    (l_sem, n_ssem, n_rsem, s_sem, r_sem, p_ssem, p_rsem, g_ssem, g_rsem, a_ssem, a_rsem,
     b_ssem, b_rsem, t_ssem, t_rsem) = sems[:15]
    sq, so, sf = sems[15:27], sems[27:32], sems[32:39]
    width = 2 * PAGE
    cols, hid = width, tdn_ref.shape[1] // 4
    ctx, rep = lax.axis_index("ctx"), lax.axis_index("rep")
    left, me, right, far = ring_neighbours()
    half_pages = pages // 2
    rows = half_pages * PAGE
    wl = tin_ref.shape[1]
    at = Place()
    bq = RepBulk(wq_ref, pkq_ref, wqx_ref, pkqx_ref, *sq)
    bo = Bulk(True, wo_ref, None, None, None, *so)
    bf = Bulk(True, wf_ref, pkf_ref, *sf)
    loads = [
        pltpu.make_async_copy(a, b, l_sem.at[k])
        for k, (a, b) in enumerate(
            [(tgu_hbm, tgu_ref), (tdn_hbm, tdn_ref), (tout_hbm, tout_ref), (tok_hbm, tok_ref)]
        )
    ]
    for load in loads:
        load.start()

    for y in range(4):
        for t in range(3):
            lane = pl.multiple_of((y * 2 + rep) * cols, cols)
            pkq_ref[y, :, pl.ds(t * cols, cols)] = tin_ref[t, :, pl.ds(lane, cols)].astype(BF16)
            lane = pl.multiple_of((y * 2 + 1 - rep) * cols, cols)
            pkqx_ref[y, :, pl.ds(t * cols, cols)] = tin_ref[
                t, pl.ds(wl // 2, wl // 2), pl.ds(lane, cols)
            ].astype(BF16)
    wq_ref[ctx, me] = pkq_ref[me]
    wqx_ref[at.z, me] = pkqx_ref[me]

    greet(
        [at.sibling(), at.same(), at.cross()]
        + [dict(ctx=at.ctx(0, dz)) for dz in (1, 2, 3)]
        + [dict(mp=left), dict(mp=right), dict(mp=far)]
    )
    bq.y_start((1, 2))
    bq.z_start(0)

    row8 = lax.broadcasted_iota(jnp.int32, (pages, PAGE), 0)
    lane8 = lax.broadcasted_iota(jnp.int32, (pages, PAGE), 1)
    upto = jnp.zeros((pages, PAGE), jnp.int32)
    alive = jnp.zeros((pages, PAGE), F32)
    so_far = jnp.int32(0)
    for b in range(pages):
        flag = live_ref[b]
        upto = jnp.where(row8 == b, so_far * PAGE + flag * (lane8 + 1), upto)
        alive = jnp.where(row8 == b, flag.astype(F32), alive)
        so_far = so_far + flag
    def num_copy(k):
        to = at.sibling() if k == 0 else at.same() if k == 4 else dict(ctx=at.ctx(0, k))
        src = num_ref.at[0 if k == 0 else 2 if k == 4 else 1]
        return remote(src, nin_ref.at[k], n_ssem, n_rsem.at[(k + 2) // 3], **to)

    num_ref[0] = jnp.zeros((pages, PAGE), jnp.int32) + so_far * PAGE
    num_copy(0).start()

    for load in loads[:3]:
        load.wait()
    wo_ref[ctx, 0] = tout_ref[...].astype(BF16)
    for y in range(4):
        for j in range(hid // PAGE):
            for t in range(2):
                pkf_ref[y, :, pl.ds(j * 2 * PAGE + t * PAGE, PAGE)] = tgu_ref[
                    t, :, pl.ds(y * hid + j * PAGE, PAGE)
                ].astype(BF16)
        pkf_ref[y, :, pl.ds(2 * hid, hid)] = tdn_ref[:, pl.ds(y * hid, hid)].astype(BF16)
    wf_ref[ctx, me] = pkf_ref[me]
    bf.x_go(0, 0)
    bo.x_go(0, 0)
    loads[3].wait()

    def norm(b):
        x = tok_ref[pt_ref[b]].astype(F32)
        scale = lax.rsqrt(jnp.mean(x * x, axis=-1, keepdims=True) + EPS)
        x_ref[pl.ds(b * PAGE, PAGE), :] = (x * scale * mgain_ref[...]).astype(BF16)

    lane1 = lax.broadcasted_iota(jnp.int32, (1, PAGE), 1) // wl

    def my_columns(read, t):
        tile = None
        for k in range(4):
            turned = pltpu.roll(read(t * 4 + k), lax.rem(wl * (k + 4) - wl * me, PAGE), 1)
            tile = turned if tile is None else jnp.where(lane1 == k, turned, tile)
        return tile

    def pick(j):
        page = pt_ref[rep * half_pages + j]
        for t in range(4):
            tile = my_columns(
                lambda c: tok_ref[page, :, pl.ds(c * PAGE, PAGE)].astype(F32), t
            )
            ord_ref[pl.ds(j * PAGE, PAGE), pl.ds(t * PAGE, PAGE)] = tile

    def project_first(part):
        near = pl.ds(pl.multiple_of(at.x * (D // 2), D // 2), D // 2)
        w = wq_ref[pl.ds(at.x * (n_ctx // 2), n_ctx // 2)].reshape(D // 2, 3 * width)
        x = x_ref[pl.ds(part * rows, rows), near]
        for t in range(3):
            acc_ref[part * 3 + t] = dot(x, w[:, t * width : (t + 1) * width])

    norm(0)
    norm(1)
    norm(2)
    bq.y_start((3,))
    bq.y_take(1)
    bq.z_start(1)
    bq.y_take(2)
    bq.z_start(2)
    num_copy(0).wait_recv()
    num_ref[1] = num_ref[0] + nin_ref[0]
    for k in (1, 2, 3):
        num_copy(k).start()
    norm(3)
    norm(4)
    bq.y_take(3)
    bq.z_start(3)
    bf.y_start((1, 2))
    bq.z_relay(0)
    bf.y_start((3,))
    norm(5)
    bq.x_take(0, 0)
    bq.z_relay(1)
    bq.z_relay(2)
    norm(6)
    bq.x_take(1, 0)
    norm(7)
    bq.x_take(2, 0)
    bq.z_relay(3)
    bo.z_start(0)
    bq.x_take(0, 1)
    bq.x_take(0, 2)
    bq.x_take(3, 0)
    there = nin_ref.at[pl.ds(1, 3)]
    remote(there, there, n_ssem, n_rsem.at[1], **at.sibling()).wait_recv()
    num_ref[2] = num_ref[1] + nin_ref[1] + nin_ref[2] + nin_ref[3]
    num_copy(4).start()
    bq.z_far(0)
    bq.x_take(1, 1)
    bq.x_take(1, 2)
    bq.z_far(1)
    bq.x_take(2, 1)
    bq.x_take(2, 2)
    bq.z_far(2)
    bq.x_take(3, 1)
    bq.x_take(3, 2)
    bq.x_take(0, 3)
    bq.z_far(3)
    bq.x_take(1, 3)
    bo.x_take(0, 0)
    bo.z_start(0, 1)
    bf.y_take(1)
    bf.z_start(1)
    bf.y_take(2)
    bq.c_take(0)
    project_first(0)
    bq.x_take(2, 3)
    bq.x_take(3, 3)
    project_first(1)
    num_copy(4).wait_recv()
    base = jnp.where(at.core == 1, nin_ref[0], 0) + jnp.where(at.x == 1, nin_ref[4], 0)
    for k in (1, 2, 3):
        base = base + jnp.where(k <= at.z, nin_ref[k], 0)
    count = jnp.zeros((pages, PAGE), F32)
    start = jnp.int32(0)
    for j in range(len_ref.shape[0]):
        count = count + jnp.where((base <= start) & (start < base + upto), 1.0, 0.0)
        start = start + len_ref[j]
    cnt_ref[pl.ds(0, 1), :] = jnp.zeros((1, PAGE), F32)
    for b in range(pages):
        cnt_ref[pl.ds(b + 1, 1), :] = count[b : b + 1, :]
    run_ref[...] = jnp.zeros_like(run_ref)
    dec_ref[...] = jnp.ones_like(dec_ref)
    row = lax.broadcasted_iota(jnp.int32, (PAGE, PAGE), 0)
    col = lax.broadcasted_iota(jnp.int32, (PAGE, PAGE), 1)
    lower = row >= col
    tri = jnp.where(lower, 1.0, 0.0).astype(BF16)
    tri = jnp.concatenate([tri, tri], axis=1)
    floor = floor_ref[...]
    bq.c_take(1)
    bf.x_take(0, 0)
    bf.flush(True)
    bo.flush(True)
    for i in (1, 2):
        bf.x_go(i, 0)

    def wide(b):
        return jnp.broadcast_to(cnt_ref[pl.ds(b + 1, 1), :], (PAGE, PAGE))

    def ends(b):
        return cnt_ref[pl.ds(b, 1), :][:, PAGE - 1 :], cnt_ref[pl.ds(b + 1, 1), :][:, PAGE - 1 :]

    def project(i):
        here2 = pl.ds(i * 256, 256)
        away = pl.ds(pl.multiple_of((1 - at.x) * (D // 2), D // 2), D // 2)
        w = wq_ref[pl.ds((1 - at.x) * (n_ctx // 2), n_ctx // 2)].reshape(D // 2, 3 * width)
        p = dot(x_ref[here2, away], w)
        pq, pf, pv = (
            p[:, t * width : (t + 1) * width] + acc_ref[i // 2 * 3 + t, pl.ds(i % 2 * 256, 256), :]
            for t in range(3)
        )
        q = pq / (1.0 + jnp.exp(-pq))
        forget = floor + (1.0 - floor) / (1.0 + jnp.exp(-pf))
        logd, key = jnp.log(forget), 1.0 - forget
        v_ref[here2, :] = pv.astype(BF16)
        for h2 in range(2):
            b = 2 * i + h2
            part = slice(h2 * PAGE, (h2 + 1) * PAGE)
            here = pl.ds(b * PAGE, PAGE)
            live = alive[b : b + 1, :]
            live = jnp.concatenate([live, live], axis=1)
            lg, kk = logd[part] * live, key[part] * live
            hi = lg.astype(BF16)
            lo = (lg - hi.astype(F32)).astype(BF16)
            c = dot(tri, jnp.concatenate([hi, lo], axis=0))
            final = c[PAGE - 1 :, :]
            before, last = ends(b)
            keep = jnp.where(wide(b).T == last, 1.0, 0.0)
            keep = jnp.concatenate([keep, keep], axis=1)
            same = jnp.where(before == last, 1.0, 0.0)
            decay = jnp.exp(final) * same
            q_ref[here, :] = (q[part] * jnp.exp(c)).astype(BF16)
            k_ref[here, :] = (kk * jnp.exp(-c)).astype(BF16)
            ke = (kk * jnp.exp(final - c) * keep).astype(BF16)
            dec = dec_ref[...]
            ctot_ref[pl.ds(b, 1), :] = dec
            dec_ref[...] = dec * decay
            for h in range(2):
                lanes = slice(h * PAGE, (h + 1) * PAGE)
                state = run_ref[h]
                st_ref[b, h] = state
                add = dot(v_ref[here, lanes], ke[:, lanes], TN)
                run_ref[h] = state * decay[:, lanes] + add

    def block_in(ref):
        tail = ref[pl.ds(PAGE, 16), :].astype(F32)
        return ref[pl.ds(0, PAGE), :].astype(F32), tail[0:1, :] + tail[1:2, :]

    def block_out(ref, block):
        state, decay = block
        ref[pl.ds(0, PAGE), :] = state.astype(BF16)
        hi = decay.astype(BF16)
        lo = (decay - hi.astype(F32)).astype(BF16)
        line = lax.broadcasted_iota(jnp.int32, (16, PAGE), 0)
        both = jnp.where(line == 0, hi.astype(F32), jnp.where(line == 1, lo.astype(F32), 0.0))
        ref[pl.ds(PAGE, 16), :] = both.astype(BF16)

    def join(early, late):
        return early[0] * late[1] + late[0], early[1] * late[1]

    def choose(flag, a, b):
        return jnp.where(flag, a[0], b[0]), jnp.where(flag, a[1], b[1])

    def state_copy(k):
        to = at.sibling() if k in (0, 5) else at.same() if k == 4 else dict(ctx=at.ctx(0, k))
        src = msg_ref.at[{0: 0, 4: 2, 5: 3}.get(k, 1)]
        return remote(src, in_ref.at[k], s_sem, r_sem.at[(0, 1, 1, 1, 2, 3)[k]], **to)

    def local_block(h):
        return run_ref[h], dec_ref[:, pl.ds(pl.multiple_of(h * PAGE, PAGE), PAGE)]

    project(0)
    project(1)
    project(2)
    bf.y_take(3)
    bf.x_go(3, 0)
    project(3)
    block_out(msg_ref.at[0], local_block(1 - at.core))
    state_copy(0).start()

    def within(b, _):
        here = pl.ds(pl.multiple_of(b * PAGE, PAGE), PAGE)
        rowwise = wide(b)
        allowed = lower & (rowwise.T == rowwise)
        for h in range(2):
            lanes = slice(h * PAGE, (h + 1) * PAGE)
            scores = dot(q_ref[here, lanes], k_ref[here, lanes], NT)
            scores = jnp.where(allowed, scores, 0.0).astype(BF16)
            mix_ref[here, lanes] = dot(scores, v_ref[here, lanes])
        return 0

    lax.fori_loop(0, 2, within, 0)
    state_copy(0).wait_recv()
    own, sib = local_block(at.core), block_in(in_ref.at[0])
    first, second = choose(at.core == 0, own, sib), choose(at.core == 0, sib, own)
    chip = join(first, second)
    block_out(msg_ref.at[1], chip)
    for k in (1, 2, 3):
        state_copy(k).start()
    bf.z_start(2)
    bf.z_start(3)
    lax.fori_loop(2, pages, within, 0)
    there = in_ref.at[pl.ds(1, 3)]
    remote(there, there, s_sem, r_sem.at[1], **at.sibling()).wait_recv()
    whole = (jnp.zeros((PAGE, PAGE), F32), jnp.ones((1, PAGE), F32))
    ahead = whole
    for z in range(at.n_z):
        there = block_in(msg_ref.at[1])
        for k in (1, 2, 3):
            there = choose(lax.rem(at.z + at.n_z - z, at.n_z) == k, block_in(in_ref.at[k]), there)
        whole = join(whole, there)
        ahead = choose(z < at.z, whole, ahead)
    block_out(msg_ref.at[2], whole)
    state_copy(4).start()
    bf.z_relay(1)
    bo.z_relay(0)
    bo.z_relay(0, 1)
    bf.x_go(1, 1)
    for j in range(half_pages):
        pick(j)
    state_copy(4).wait_recv()
    before = choose(at.x == 1, block_in(in_ref.at[4]), (jnp.zeros((PAGE, PAGE), F32), jnp.ones((1, PAGE), F32)))
    enter0 = join(before, ahead)
    enter1 = join(enter0, first)
    block_out(msg_ref.at[3], choose(at.core == 0, enter1, enter0))
    state_copy(5).start()
    run_ref[at.core] = choose(at.core == 0, enter0, enter1)[0]
    state_copy(5).wait_recv()
    run_ref[1 - at.core] = block_in(in_ref.at[5])[0]

    def outputs(b, dst, dst_row, dst_lane):
        here = pl.ds(pl.multiple_of(b * PAGE, PAGE), PAGE)
        before, _ = ends(b)
        open_rows = wide(b).T == before
        total = ctot_ref[pl.ds(b, 1), :]
        for h in range(2):
            lanes = slice(h * PAGE, (h + 1) * PAGE)
            state = st_ref[b, h] + total[:, lanes] * run_ref[h]
            old = dot(q_ref[here, lanes], state.astype(BF16), NT)
            mixed = mix_ref[here, lanes] + jnp.where(open_rows, old, 0.0)
            scale = lax.rsqrt(jnp.mean(mixed * mixed, axis=-1, keepdims=True) + EPS)
            dst[dst_row, pl.ds(dst_lane + h * PAGE, PAGE)] = (mixed * scale).astype(BF16)

    def lane_of(owner, which):
        return pl.multiple_of((owner * 2 + which) * width, width)

    def swap_out(k, n):
        to = at.same() if k == 0 else at.cross()
        return remote(
            oth_ref.at[pl.ds((2 * n + k) * PAGE, PAGE), :], via_ref.at[k, n],
            p_ssem, p_rsem.at[2 * k + n], **to,
        )

    def swap_on(k, n):
        to = at.cross() if k == 0 else at.same()
        which = rep if k == 0 else 1 - rep
        dst = head_ref.at[pl.ds((2 * n + k) * PAGE, PAGE), pl.ds(lane_of(me, which), width)]
        return remote(
            via_ref.at[k, n], dst, p_ssem, p_rsem.at[4 + n], **to
        )

    for n in range(2):
        for k in range(2):
            j = 2 * n + k
            outputs((1 - rep) * half_pages + j, oth_ref, pl.ds(j * PAGE, PAGE), 0)
            swap_out(k, n).start()
    bf.flush(False)
    bo.flush(False)
    bf.z_relay(2)
    bf.z_start(0)
    mine = lane_of(me, rep)
    part = rows // 2

    def own_half(j, _):
        outputs(rep * half_pages + j, head_ref, pl.ds(pl.multiple_of(j * PAGE, PAGE), PAGE), mine)
        return 0

    def view(which, n):
        return lambda owner, r, count: head_ref.at[
            pl.ds(n * part + r, count), pl.ds(lane_of(owner, which), width)
        ]

    three = head_ref.at[pl.ds(0, part), pl.ds(0, 3 * width)]
    ring_a = [Ring(view(rep, n), part, three, g_ssem, g_rsem, n) for n in range(2)]
    ring_b = [Ring(view(1 - rep, n), part, three, g_ssem, g_rsem, 2 + n) for n in range(2)]
    ring_x = [
        Ring(
            lambda owner, r, count, n=n: xall_ref.at[owner, pl.ds(n * part + r, count), :],
            part, xall_ref.at[pl.ds(0, 3), pl.ds(0, part), :], a_ssem, a_rsem, n,
        )
        for n in range(2)
    ]
    for n in range(2):
        lax.fori_loop(n * (half_pages // 2), (n + 1) * (half_pages // 2), own_half, 0)
        ring_a[n].start()
    for n in range(2):
        for k in range(2):
            swap_out(k, n).wait_recv()
            swap_on(k, n).start()
    bf.x_go(1, 2)
    bf.x_go(2, 1)
    bf.x_go(2, 2)
    bf.z_start(0, 1)
    ring_a[0].relay()
    remote(via_ref.at[0], via_ref.at[0], p_ssem, p_rsem.at[4], **at.sibling()).wait_recv()
    ring_b[0].start()
    ring_a[1].relay()
    remote(via_ref.at[0], via_ref.at[0], p_ssem, p_rsem.at[5], **at.sibling()).wait_recv()
    ring_b[0].relay()
    ring_b[1].start()
    bo.z_far(0)
    bo.z_far(0, 1)
    bf.z_relay(3)
    bf.z_far(1)
    bf.x_go(1, 3)
    ring_b[1].relay()
    bf.z_far(2)
    bf.x_go(2, 3)
    bf.x_go(3, 1)
    bf.x_go(3, 2)
    bo.c_take(0)
    for i in (1, 2, 3):
        bf.x_take(i, 0)
    gain = jnp.concatenate(
        [my_columns(lambda c: jnp.broadcast_to(fgain_ref[:, pl.ds(c * PAGE, PAGE)], (8, PAGE)), t)[0:1] for t in range(4)],
        axis=1,
    )

    def ss_copy(n, k, owner):
        ref = ss_ref.at[n, owner]
        to = left if k == 1 else right
        return remote(ref, ref, b_ssem.at[n], b_rsem.at[3 * n + k], mp=to)

    def out_proj(n):
        here = pl.ds(n * part, part)
        res = ord_ref[here, :] + dot(head_ref[here, :], wo_ref[...].reshape(4 * PAGE, D), NT)
        sqr = res * res
        hi = sqr.astype(BF16)
        lo = (sqr - hi.astype(F32)).astype(BF16)
        ones = jnp.ones((8, sqr.shape[1]), BF16)
        ss_ref[n, me] = dot(ones, hi, NT) + dot(ones, lo, NT)
        ss_copy(n, 0, me).start()
        ss_copy(n, 1, me).start()
        xall_ref[me, here, :] = (res * gain).astype(BF16)
        ring_x[n].start()
        for t in range(4):
            tile = res[:, t * PAGE : (t + 1) * PAGE]
            for k in range(4):
                turned = pltpu.roll(tile, lax.rem(wl * (4 - k) + wl * me, PAGE), 1)
                res_ref[here, pl.ds((t * 4 + k) * PAGE, PAGE)] = jnp.where(lane1 == me, turned, 0.0)

    def x_relay(n):
        ss_copy(n, 0, left).wait_recv()
        ss_copy(n, 2, left).start()
        ss_copy(n, 1, right).wait_recv()
        ring_x[n].relay()

    def x_rest(n):
        ring_x[n].near()
        ss_copy(n, 2, far).wait_recv()
        ring_x[n].finish()
        ss = ss_ref[n, 0]
        for y in range(1, 4):
            ss = ss + ss_ref[n, y]
        scale = lax.rsqrt(ss / D + EPS)[0:1, :]
        rs_ref[pl.ds(n * part, part), :] = jnp.broadcast_to(scale, (PAGE, part)).T

    for ring in (ring_a[0], ring_b[0]):
        ring.near()
        ring.finish()
    out_proj(0)
    bf.z_relay(0, 0)
    for ring in (ring_a[1], ring_b[1]):
        ring.near()
        ring.finish()
    out_proj(1)
    x_relay(0)
    bf.z_far(3)
    bf.x_go(3, 3)
    bf.z_relay(0, 1)
    bf.x_take(1, 1)
    bf.x_take(1, 2)
    bf.x_take(2, 1)
    bf.x_take(2, 2)
    x_relay(1)
    bf.z_far(0, 0)
    bf.x_take(1, 3)
    bf.x_take(2, 3)
    bf.x_take(3, 1)
    bf.x_take(3, 2)
    bf.x_take(3, 3)
    bf.z_far(0, 1)
    bq.drain()
    bo.drain()
    remote(v_ref, v_ref, p_ssem, p_rsem.at[0], **at.sibling()).wait_send()
    remote(in_ref, in_ref, s_sem, r_sem.at[0], **at.sibling()).wait_send()
    remote(nin_ref, nin_ref, n_ssem, n_rsem.at[0], **at.sibling()).wait_send()
    x_rest(0)
    for i in range(4):
        bf.c_take(i)

    def gate_up(n, first, last):
        here = pl.ds(n * part, part)
        for j in range(first, last):
            lanes = pl.ds(j * 256, 256)
            acc = None
            for y in range(4):
                term = dot(xall_ref[y, here, :], wf_ref[:, y, :, lanes].reshape(D // 4, 256))
                acc = term if acc is None else acc + term
            rs = rs_ref[here, :]
            g, u = acc[:, :PAGE] * rs, acc[:, PAGE:] * rs
            hid_ref[here, pl.ds(j * PAGE, PAGE)] = (g / (1.0 + jnp.exp(-g)) * u).astype(BF16)

    def block_of(owner):
        return pl.ds(pl.multiple_of(owner * 4 * PAGE, PAGE), 4 * PAGE)

    def partial(n, owner):
        here = pl.ds(n * part, part)
        w = wf_ref[pl.ds(owner * 4, 4), :, :, pl.ds(2 * hid, hid)].reshape(4 * PAGE, hid)
        res_ref[here, block_of(owner)] = res_ref[here, block_of(owner)] + dot(hid_ref[here, :], w, NT)

    half = part // 2

    class Reduce:
        def __init__(self, n):
            self.n = n
            self.upper, self.under = pl.ds(n * part, half), pl.ds(n * part + half, half)
            self.far_r = self.hop(0, self.upper, 0, 0, right)
            self.far_l = self.hop(0, self.under, 1, 1, left)
            self.near_r1 = self.hop(1, self.under, 2, 2, right)
            self.near_r2 = self.hop(1, self.upper, 2, 3, right)
            self.near_l1 = self.hop(2, self.upper, 3, 4, left)
            self.near_l2 = self.hop(2, self.under, 3, 5, left)

        def hop(self, slot, where, to_slot, k, to):
            return remote(
                send_ref.at[slot, where, :], rin_ref.at[to_slot, where, :],
                t_ssem.at[self.n], t_rsem.at[3 * self.n + min(k, 2)], mp=to,
            )

        def first(self):
            here = pl.ds(self.n * part, part)
            partial(self.n, far)
            send_ref[0, here, :] = res_ref[here, block_of(far)].astype(BF16)
            self.far_r.start()
            self.far_l.start()
            partial(self.n, right)
            send_ref[1, self.under, :] = res_ref[self.under, block_of(right)].astype(BF16)
            self.near_r1.start()
            partial(self.n, left)
            send_ref[2, self.upper, :] = res_ref[self.upper, block_of(left)].astype(BF16)
            self.near_l1.start()

        def second(self):
            self.far_r.wait_recv()
            send_ref[1, self.upper, :] = (
                res_ref[self.upper, block_of(right)] + rin_ref[0, self.upper, :].astype(F32)
            ).astype(BF16)
            self.near_r2.start()
            self.far_l.wait_recv()
            send_ref[2, self.under, :] = (
                res_ref[self.under, block_of(left)] + rin_ref[1, self.under, :].astype(F32)
            ).astype(BF16)
            self.near_l2.start()

        def last(self):
            two = rin_ref.at[pl.ds(0, 2), pl.ds(0, part), :]
            remote(two, two, t_ssem.at[self.n], t_rsem.at[3 * self.n + 2], mp=right).wait_recv()
            for p in range(half_pages // 2):
                page = self.n * (half_pages // 2) + p
                r = pl.ds(page * PAGE, PAGE)
                total = (
                    res_ref[r, block_of(me)] + rin_ref[2, r, :].astype(F32)
                    + rin_ref[3, r, :].astype(F32)
                )
                out_ref[r, :] = jnp.where(
                    live_ref[rep * half_pages + page] == 1, total, 0.0
                ).astype(BF16)

        def drain(self):
            three = send_ref.at[:, pl.ds(0, part), :]
            remote(three, three, t_ssem.at[self.n], t_rsem.at[3 * self.n], mp=right).wait_send()

    reduce = [Reduce(n) for n in range(2)]
    tiles = hid // PAGE
    gate_up(0, 0, tiles)
    reduce[0].first()
    x_rest(1)
    gate_up(1, 0, tiles // 2)
    reduce[0].second()
    gate_up(1, tiles // 2, tiles)
    reduce[1].first()
    partial(0, me)
    partial(1, me)
    reduce[1].second()
    bf.drain()
    for n in range(2):
        three = ss_ref.at[n, pl.ds(0, 3)]
        remote(three, three, b_ssem.at[n], b_rsem.at[0], mp=right).wait_send()
    reduce[0].last()
    reduce[1].last()
    for n in range(2):
        reduce[n].drain()


VM = pl.BlockSpec(memory_space=pltpu.VMEM)
HB = pl.BlockSpec(memory_space=pl.ANY)
SM = pl.BlockSpec(memory_space=pltpu.SMEM)


def shards(
    token_pages, page_table, live_flags, lengths, decay_floor, mixer_gain, feed_gain,
    trainer_mixer_in, trainer_mixer_out, trainer_gate_up, trainer_down,
):
    n_ctx = lax.axis_size("ctx")
    pages, page, _ = token_pages.shape
    tokens, half = pages * page, pages * page // 2
    wl = trainer_mixer_in.shape[1]
    cols = decay_floor.shape[0]
    hid = trainer_gate_up.shape[2] // 4
    block = D // 4
    dma = pltpu.SemaphoreType.DMA

    def bulk_sems(n, y):
        near = [dma(()), dma((3,))] if y else []
        return near + [dma(()), dma((n, 2)), dma((n, 2)), dma((n, 4)), dma((n,))]

    return pl.pallas_call(
        functools.partial(layer_kernel, n_ctx, pages),
        out_shape=jax.ShapeDtypeStruct((half, block), BF16),
        in_specs=[SM, SM, SM] + [VM] * 4 + [HB] * 4,
        out_specs=VM,
        scratch_shapes=[
            pltpu.VMEM((pages, page, D), BF16),
            pltpu.VMEM((wl, D), F32),
            pltpu.VMEM((2, wl, 4 * hid), F32),
            pltpu.VMEM((wl, 4 * hid), F32),
            pltpu.VMEM((n_ctx, 4, wl, 3 * cols), BF16),
            pltpu.VMEM((4, 4, wl // 2, 3 * cols), BF16),
            pltpu.VMEM((n_ctx, 1, wl, D), BF16),
            pltpu.VMEM((n_ctx, 4, wl, 3 * hid), BF16),
            pltpu.VMEM((4, wl, 3 * cols), BF16),
            pltpu.VMEM((4, wl // 2, 3 * cols), BF16),
            pltpu.VMEM((4, wl, 3 * hid), BF16),
            pltpu.VMEM((tokens, D), BF16),
            pltpu.VMEM((half, block), F32),
            pltpu.VMEM((tokens, cols), BF16),
            pltpu.VMEM((tokens, cols), BF16),
            pltpu.VMEM((tokens, cols), BF16),
            pltpu.VMEM((pages, cols), F32),
            pltpu.VMEM((16, PAGE), F32),
            pltpu.VMEM((pages, 2, PAGE, PAGE), F32),
            pltpu.VMEM((1, cols), F32),
            pltpu.VMEM((2, PAGE, PAGE), F32),
            pltpu.VMEM((tokens, cols), F32),
            pltpu.VMEM((4, PAGE + 16, PAGE), BF16),
            pltpu.VMEM((6, PAGE + 16, PAGE), BF16),
            pltpu.VMEM((3, pages, PAGE), jnp.int32),
            pltpu.VMEM((5, pages, PAGE), jnp.int32),
            pltpu.VMEM((half, cols), BF16),
            pltpu.VMEM((2, 2, half // 4, cols), BF16),
            pltpu.VMEM((half, D), BF16),
            pltpu.VMEM((4, half, block), BF16),
            pltpu.VMEM((2, 4, 8, half // 2), F32),
            pltpu.VMEM((half, D), F32),
            pltpu.VMEM((half, hid), BF16),
            pltpu.VMEM((half, PAGE), F32),
            pltpu.VMEM((6, half, 256), F32),
            pltpu.VMEM((3, half, block), BF16),
            pltpu.VMEM((4, half, block), BF16),
            dma((4,)), dma(()), dma((3,)), dma(()), dma((4,)),
            dma(()), dma((6,)), dma((4,)), dma((4, 3)), dma((2,)), dma((2, 3)),
            dma((2,)), dma((6,)), dma((2,)), dma((6,)),
        ]
        + [dma(()), dma((3,)), dma(()), dma((4,)), dma((4,))]
        + bulk_sems(4, True) + bulk_sems(1, False) + bulk_sems(4, True),
        compiler_params=pltpu.CompilerParams(
            collective_id=0, has_side_effects=True, vmem_limit_bytes=VMEM_LIMIT
        ),
        name="layer",
    )(
        page_table, live_flags, lengths, decay_floor.reshape(1, cols),
        mixer_gain.reshape(1, D), feed_gain.reshape(1, D),
        trainer_mixer_in, token_pages, trainer_mixer_out.T, trainer_gate_up, trainer_down.T,
    )


def solution(mesh):
    in_specs = (
        P("ctx", None, None),
        P("ctx"),
        P("ctx"),
        P(),
        P(("mp", "rep")),
        P(),
        P(),
        P(None, ("ctx", "mp"), None),
        P(None, ("ctx", "mp")),
        P(None, ("ctx", "mp"), None),
        P(None, ("ctx", "mp")),
    )
    out_specs = P(("ctx", "rep"), "mp")
    return jax.shard_map(shards, mesh=mesh, in_specs=in_specs, out_specs=out_specs, check_vma=False)
```

time: 142 us -> 108 us (0.76)
  Pallas kernels: 140 us -> 106 us
    pallas_call x1, Pallas kernels: 140 us -> 106 us  [shards(): pl.pallas_call(functools.partial(layer_kernel, n_ctx, pages), out_shape=j...]
where the time goes in v4:
time: 108 us
  Pallas kernels  106 us (98%)
  local copies, waits for them, and re-layouts  1.87 us (2%)
    pallas_call x1, Pallas kernels, shards(): pl.pallas_call(functools.partial(layer_kernel, n_ctx, pages), out_shape=j...  106 us

profile of v4, /device:TPU:1, one launch (start us, length us, event | category | flops | bytes accessed | tf_op | source)
XLA Modules:
  0.0 108.3 jit_solution(225951748737536069)
XLA Ops:
  0.0 106.4 %layer.1 = bf16[512,512]{1,0:T(8,128)(2,1)} custom-call(s32[8]{0:T(128)} %pt_ref.1, s32[8]{0:T(128)} %live_ref.1, s32[32]{0:T(128)} %len_ref.1, f32[1,256]{1,0:T(1,128)} %bitcast.9, f32[1,2048]{1,0:T(1,128)} %bitcast.7, f32[1,2048]{1,0:T(1,128)} %bitcast.8, f32[3,32,2048]{2,1,0:T(8,128)} %tin_ref.1, bf16[8,128,2048]{2,1,0:T(8,128)(2,1)} %tok_hbm.1, ...), custom_call_target="tpu_custom_call" | custom-call | tf_op jit(solution)/shard_map/layer/pallas_call | solution.py:932
  106.4 1.9 %copy.13 = bf16[512,512]{1,0:T(8,128)(2,1)} copy(bf16[512,512]{1,0:T(8,128)(2,1)} %layer.1) | data formatting | bytes 1048576

commit v5 on v4

--- a/solution.py
+++ b/solution.py
@@ -299,10 +299,10 @@
 
 def layer_kernel(
     n_ctx, pages,
-    pt_ref, live_ref, len_ref, floor_ref, mgain_ref, fgain_ref,
-    tin_ref, tok_hbm, tout_hbm, tgu_hbm, tdn_hbm,
+    pt_ref, live_ref, len_ref, floor_hbm, mgain_hbm, fgain_hbm,
+    tin_hbm, tok_hbm, tout_hbm, tgu_hbm, tdn_hbm,
     out_ref,
-    tok_ref, tout_ref, tgu_ref, tdn_ref,
+    tok_ref, tout_ref, tgu_ref, tdn_ref, tin_ref, floor_ref, mgain_ref, fgain_ref,
     wq_ref, wqx_ref, wo_ref, wf_ref, pkq_ref, pkqx_ref, pkf_ref, x_ref, ord_ref,
     q_ref, k_ref, v_ref, ctot_ref, cnt_ref, st_ref, dec_ref, run_ref, mix_ref,
     msg_ref, in_ref, num_ref, nin_ref, oth_ref, via_ref, head_ref, xall_ref, ss_ref, res_ref,
@@ -326,12 +326,22 @@
     loads = [
         pltpu.make_async_copy(a, b, l_sem.at[k])
         for k, (a, b) in enumerate(
-            [(tgu_hbm, tgu_ref), (tdn_hbm, tdn_ref), (tout_hbm, tout_ref), (tok_hbm, tok_ref)]
+            [
+                (tin_hbm, tin_ref), (tgu_hbm, tgu_ref), (tdn_hbm, tdn_ref), (tout_hbm, tout_ref),
+                (mgain_hbm, mgain_ref), (floor_hbm, floor_ref), (fgain_hbm, fgain_ref),
+                (tok_hbm, tok_ref),
+            ]
         )
     ]
     for load in loads:
         load.start()
 
+    greet(
+        [at.sibling(), at.same(), at.cross()]
+        + [dict(ctx=at.ctx(0, dz)) for dz in (1, 2, 3)]
+        + [dict(mp=left), dict(mp=right), dict(mp=far)]
+    )
+    loads[0].wait()
     for y in range(4):
         for t in range(3):
             lane = pl.multiple_of((y * 2 + rep) * cols, cols)
@@ -343,11 +353,6 @@
     wq_ref[ctx, me] = pkq_ref[me]
     wqx_ref[at.z, me] = pkqx_ref[me]
 
-    greet(
-        [at.sibling(), at.same(), at.cross()]
-        + [dict(ctx=at.ctx(0, dz)) for dz in (1, 2, 3)]
-        + [dict(mp=left), dict(mp=right), dict(mp=far)]
-    )
     bq.y_start((1, 2))
     bq.z_start(0)
 
@@ -369,7 +374,7 @@
     num_ref[0] = jnp.zeros((pages, PAGE), jnp.int32) + so_far * PAGE
     num_copy(0).start()
 
-    for load in loads[:3]:
+    for load in loads[1:4]:
         load.wait()
     wo_ref[ctx, 0] = tout_ref[...].astype(BF16)
     for y in range(4):
@@ -382,7 +387,8 @@
     wf_ref[ctx, me] = pkf_ref[me]
     bf.x_go(0, 0)
     bo.x_go(0, 0)
-    loads[3].wait()
+    for load in loads[4:]:
+        load.wait()
 
     def norm(b):
         x = tok_ref[pt_ref[b]].astype(F32)
@@ -932,13 +938,17 @@
     return pl.pallas_call(
         functools.partial(layer_kernel, n_ctx, pages),
         out_shape=jax.ShapeDtypeStruct((half, block), BF16),
-        in_specs=[SM, SM, SM] + [VM] * 4 + [HB] * 4,
+        in_specs=[SM, SM, SM] + [HB] * 8,
         out_specs=VM,
         scratch_shapes=[
             pltpu.VMEM((pages, page, D), BF16),
             pltpu.VMEM((wl, D), F32),
             pltpu.VMEM((2, wl, 4 * hid), F32),
             pltpu.VMEM((wl, 4 * hid), F32),
+            pltpu.VMEM((3, wl, D), F32),
+            pltpu.VMEM((1, cols), F32),
+            pltpu.VMEM((1, D), F32),
+            pltpu.VMEM((1, D), F32),
             pltpu.VMEM((n_ctx, 4, wl, 3 * cols), BF16),
             pltpu.VMEM((4, 4, wl // 2, 3 * cols), BF16),
             pltpu.VMEM((n_ctx, 1, wl, D), BF16),
@@ -972,7 +982,7 @@
             pltpu.VMEM((6, half, 256), F32),
             pltpu.VMEM((3, half, block), BF16),
             pltpu.VMEM((4, half, block), BF16),
-            dma((4,)), dma(()), dma((3,)), dma(()), dma((4,)),
+            dma((8,)), dma(()), dma((3,)), dma(()), dma((4,)),
             dma(()), dma((6,)), dma((4,)), dma((4, 3)), dma((2,)), dma((2, 3)),
             dma((2,)), dma((6,)), dma((2,)), dma((6,)),
         ]

time: 108 us -> 108 us (level); the launches traced: 108 us -> 107 us
    pallas_call x1, Pallas kernels: 106 us -> 105 us  [shards(): pl.pallas_call(functools.partial(layer_kernel, n_ctx, pages), out_shape=j...]
where the time goes in v5:
time: 108 us; the launch traced here: 107 us
  Pallas kernels  105 us (97%)
  local copies, waits for them, and re-layouts  1.87 us (2%)
    pallas_call x1, Pallas kernels, shards(): pl.pallas_call(functools.partial(layer_kernel, n_ctx, pages), out_shape=j...  105 us

profile of v5, /device:TPU:1, one launch (start us, length us, event | category | flops | bytes accessed | tf_op | source)
XLA Modules:
  0.0 106.5 jit_solution(13097448411328634886)
XLA Ops:
  0.0 104.7 %layer.1 = bf16[512,512]{1,0:T(8,128)(2,1)} custom-call(s32[8]{0:T(128)} %pt_ref.1, s32[8]{0:T(128)} %live_ref.1, s32[32]{0:T(128)} %len_ref.1, f32[1,256]{1,0:T(1,128)} %bitcast.9, f32[1,2048]{1,0:T(1,128)} %bitcast.7, f32[1,2048]{1,0:T(1,128)} %bitcast.8, f32[3,32,2048]{2,1,0:T(8,128)} %tin_hbm.1, bf16[8,128,2048]{2,1,0:T(8,128)(2,1)} %tok_hbm.1, ...), custom_call_target="tpu_custom_call" | custom-call | tf_op jit(solution)/shard_map/layer/pallas_call | solution.py:938
  104.7 1.9 %copy.13 = bf16[512,512]{1,0:T(8,128)(2,1)} copy(bf16[512,512]{1,0:T(8,128)(2,1)} %layer.1) | data formatting | bytes 1048576

commit v6 on v5

--- a/solution.py
+++ b/solution.py
@@ -625,7 +625,6 @@
     bf.z_relay(1)
     bo.z_relay(0)
     bo.z_relay(0, 1)
-    bf.x_go(1, 1)
     for j in range(half_pages):
         pick(j)
     state_copy(4).wait_recv()
@@ -707,6 +706,7 @@
         for k in range(2):
             swap_out(k, n).wait_recv()
             swap_on(k, n).start()
+    bf.x_go(1, 1)
     bf.x_go(1, 2)
     bf.x_go(2, 1)
     bf.x_go(2, 2)

time: 108 us -> 108 us (level)
  no operation moved by 1% of the time
where the time goes in v6:
time: 108 us; the launch traced here: 106 us
  Pallas kernels  105 us (97%)
  local copies, waits for them, and re-layouts  1.87 us (2%)
    pallas_call x1, Pallas kernels, shards(): pl.pallas_call(functools.partial(layer_kernel, n_ctx, pages), out_shape=j...  105 us

profile of v6, /device:TPU:1, one launch (start us, length us, event | category | flops | bytes accessed | tf_op | source)
XLA Modules:
  0.0 106.4 jit_solution(1310919896179739507)
XLA Ops:
  0.0 104.6 %layer.1 = bf16[512,512]{1,0:T(8,128)(2,1)} custom-call(s32[8]{0:T(128)} %pt_ref.1, s32[8]{0:T(128)} %live_ref.1, s32[32]{0:T(128)} %len_ref.1, f32[1,256]{1,0:T(1,128)} %bitcast.9, f32[1,2048]{1,0:T(1,128)} %bitcast.7, f32[1,2048]{1,0:T(1,128)} %bitcast.8, f32[3,32,2048]{2,1,0:T(8,128)} %tin_hbm.1, bf16[8,128,2048]{2,1,0:T(8,128)(2,1)} %tok_hbm.1, ...), custom_call_target="tpu_custom_call" | custom-call | tf_op jit(solution)/shard_map/layer/pallas_call | solution.py:938
  104.6 1.9 %copy.13 = bf16[512,512]{1,0:T(8,128)(2,1)} copy(bf16[512,512]{1,0:T(8,128)(2,1)} %layer.1) | data formatting | bytes 1048576
